TPU v7x, 256 devices: a whole 4x4x8 slice. The times are simulated.
256 devices in a mesh: px: 32 (over z, x), py: 8 (over y, core).
Axes of the slice: x: 4, y: 4, z: 8, core: 2. Of those that a mesh axis runs over, the one named last changes fastest.
Arguments:
- field: float32 [512, 512, 1024], P('px', 'py'), may hold values from -120 to 120
- seeds_first: int32 [512, 128], replicated, may hold values from -64 to 63
- seeds_second: int32 [512, 128], replicated, may hold values from -64 to 63
Outputs:
- basis_first: float32 [512, 128], replicated
- basis_second: float32 [512, 128], replicated
- core_tensor: float32 [128, 128, 1024], P('px', 'py')
All inputs are finite; a program needn't handle non-finite values.
Results may differ from a plain program's by a relative error of at most 0.0003.
Values sent between devices are 32-bit elements; how exact they have to be, the bound alone decides.
No kernel may reach another device: no remote copies, remote signals or barrier semaphores. Data moves between devices by JAX's collectives and lax.ppermute only.
A program may use at most 128 MiB of HBM per device.

v0:
```python
import jax
import jax.numpy as jnp
from jax import lax
from jax.sharding import PartitionSpec as P

ITERS = 4


def orthonormal(matrix):
    inner = jnp.dot(matrix.T, matrix, precision=lax.Precision.HIGHEST)
    factor = jnp.linalg.cholesky(inner)
    return jax.scipy.linalg.solve_triangular(factor, matrix.T, lower=True).T


def leading_basis(partial_gram, seeds):
    basis = orthonormal(seeds.astype(jnp.float32))
    gram = lax.psum(partial_gram, ("px", "py"))
    for sweep in range(ITERS):
        basis = orthonormal(jnp.dot(gram, basis, precision=lax.Precision.HIGHEST))
    return basis


def local(field, seeds_first, seeds_second):
    fibers = lax.all_to_all(field, "px", split_axis=1, concat_axis=0, tiled=True)
    whole_first = fibers.shape[0]
    flattened = fibers.reshape(whole_first, -1)
    partial_first = jnp.dot(flattened, flattened.T, precision=lax.Precision.HIGHEST)
    basis_first = leading_basis(partial_first, seeds_first)
    rank_size = basis_first.shape[1]
    reduced = jnp.dot(basis_first.T, flattened, precision=lax.Precision.HIGHEST)
    reduced = reduced.reshape(rank_size, fibers.shape[1], fibers.shape[2])
    slab_fibers = lax.all_to_all(
        lax.all_to_all(reduced, "px", split_axis=0, concat_axis=1, tiled=True),
        "py",
        split_axis=2,
        concat_axis=1,
        tiled=True,
    )
    whole_second = slab_fibers.shape[1]
    turned = jnp.transpose(slab_fibers, (1, 0, 2)).reshape(whole_second, -1)
    partial_second = jnp.dot(turned, turned.T, precision=lax.Precision.HIGHEST)
    basis_second = leading_basis(partial_second, seeds_second)
    core_tensor = jnp.einsum(
        "jb,ajp->abp", basis_second, slab_fibers, precision=lax.Precision.HIGHEST
    )
    core_tensor = lax.all_to_all(core_tensor, "py", split_axis=1, concat_axis=2, tiled=True)
    return (basis_first, basis_second, core_tensor)


def solution(mesh):
    placed = (P("px", "py", None), P(), P())
    return jax.shard_map(
        local,
        mesh=mesh,
        in_specs=placed,
        out_specs=(P(), P(), P("px", "py", None)),
        check_vma=False,
    )
```

profile of v0, /device:TPU:1, one launch (start us, length us, event | category | flops | bytes accessed | tf_op | source)
XLA Modules:
  0.0 948.8 jit_solution(8441352326940024443)
XLA Ops:
  7.2 6.6 copy.84
  13.8 12.1 %all-to-all-start = ((f32[16,64,1024]{2,0,1:T(8,128)}), f32[16,64,1024]{2,0,1:T(8,128)}, u32[]{:S(2)}, u32[]{:S(2)}) async-start(f32[16,64,1024]{2,0,1:T(8,128)} %copy.84), calls=%async_computation | async-start | bytes 8388608 | tf_op jit(solution)/shard_map/all_to_all | solution.py:24
  27.0 11.7 %cholesky.164 = f32[128,128]{1,0:T(8,128)S(1)} custom-call(f32[128,128]{1,0:T(8,128)S(1)} %fusion.58), custom_call_target="Cholesky" | custom-call | tf_op jit(solution)/shard_map/jit(cholesky)/cholesky | solution.py:11
  38.7 80.2 %all-to-all-done = f32[16,64,1024]{2,0,1:T(8,128)} async-done(((f32[16,64,1024]{2,0,1:T(8,128)}), f32[16,64,1024]{2,0,1:T(8,128)}, u32[]{:S(2)}, u32[]{:S(2)}) %all-to-all-start) | async-done | bytes 4194336 | tf_op jit(solution)/shard_map/all_to_all | solution.py:24
  118.9 5.5 copy.85
  124.5 2.0 copy.112
  126.4 1.9 copy-done
  128.4 8.4 fusion.67
  138.1 9.8 %custom-call.14 = f32[1,128,128]{1,2,0:T(8,128)S(1)} custom-call(f32[1,128,128]{2,1,0:T(8,128)S(1)} %fusion.29), custom_call_target="InvertDiagBlocksLowerTriangular" | custom-call | tf_op jit(solution)/shard_map/jit(_solve_triangular)/triangular_solve | solution.py:12
  148.3 5.5 copy.91
  153.9 237.6 %all-reduce.3.cloned.1.call-done = f32[512,512]{1,0:T(8,128)} async-done(((f32[512,512]{1,0:T(8,128)}), f32[512,512]{1,0:T(8,128)}) %all-reduce.3.cloned.1.call-update) | async-done | bytes 1048592 | tf_op jit(solution)/shard_map/psum | solution.py:17
  391.5 2.3 fusion.68
  394.5 11.7 %cholesky.175 = f32[128,128]{1,0:T(8,128)S(1)} custom-call(f32[128,128]{1,0:T(8,128)S(1)} %fusion.56), custom_call_target="Cholesky" | custom-call | tf_op jit(solution)/shard_map/jit(cholesky)/cholesky | solution.py:11
  407.6 9.8 %custom-call.15 = f32[1,128,128]{1,2,0:T(8,128)S(1)} custom-call(f32[1,128,128]{2,1,0:T(8,128)S(1)} %fusion.30), custom_call_target="InvertDiagBlocksLowerTriangular" | custom-call | tf_op jit(solution)/shard_map/jit(_solve_triangular)/triangular_solve | solution.py:12
  417.8 2.2 fusion.70
  420.8 11.9 %cholesky.186 = f32[128,128]{1,0:T(8,128)S(1)} custom-call(f32[128,128]{1,0:T(8,128)S(1)} %fusion.54), custom_call_target="Cholesky" | custom-call | tf_op jit(solution)/shard_map/jit(cholesky)/cholesky | solution.py:11
  434.0 9.8 %custom-call.16 = f32[1,128,128]{1,2,0:T(8,128)S(1)} custom-call(f32[1,128,128]{2,1,0:T(8,128)S(1)} %fusion.31), custom_call_target="InvertDiagBlocksLowerTriangular" | custom-call | tf_op jit(solution)/shard_map/jit(_solve_triangular)/triangular_solve | solution.py:12
  444.3 1.0 fusion.72
  446.0 11.7 %cholesky.197 = f32[128,128]{1,0:T(8,128)S(1)} custom-call(f32[128,128]{1,0:T(8,128)S(1)} %fusion.52), custom_call_target="Cholesky" | custom-call | tf_op jit(solution)/shard_map/jit(cholesky)/cholesky | solution.py:11
  459.0 9.8 %custom-call.17 = f32[1,128,128]{1,2,0:T(8,128)S(1)} custom-call(f32[1,128,128]{2,1,0:T(8,128)S(1)} %fusion.32), custom_call_target="InvertDiagBlocksLowerTriangular" | custom-call | tf_op jit(solution)/shard_map/jit(_solve_triangular)/triangular_solve | solution.py:12
  469.2 1.4 fusion.74
  471.3 11.7 %cholesky.208 = f32[128,128]{1,0:T(8,128)S(1)} custom-call(f32[128,128]{1,0:T(8,128)S(1)} %fusion.50), custom_call_target="Cholesky" | custom-call | tf_op jit(solution)/shard_map/jit(cholesky)/cholesky | solution.py:11
  484.4 9.8 %custom-call.18 = f32[1,128,128]{1,2,0:T(8,128)S(1)} custom-call(f32[1,128,128]{2,1,0:T(8,128)S(1)} %fusion.33), custom_call_target="InvertDiagBlocksLowerTriangular" | custom-call | tf_op jit(solution)/shard_map/jit(_solve_triangular)/triangular_solve | solution.py:12
  494.6 6.5 fusion.11
  502.1 35.5 %all_to_all.69 = f32[128,2,1024]{2,1,0:T(2,128)S(1)} all-to-all(f32[128,2,1024]{2,1,0:T(2,128)S(1)} %copy.92), channel_id=1, replica_groups=mesh['px'=32,'py'=8] {'px'}, dimensions={0} | all-to-all | bytes 2097152 | tf_op jit(solution)/shard_map/all_to_all | solution.py:33
  539.0 2.8 reshape.25
  541.8 6.2 all-to-all-start.2
  548.8 11.7 %cholesky.219 = f32[128,128]{1,0:T(8,128)S(1)} custom-call(f32[128,128]{1,0:T(8,128)S(1)} %fusion.48), custom_call_target="Cholesky" | custom-call | tf_op jit(solution)/shard_map/jit(cholesky)/cholesky | solution.py:11
  560.5 2.6 all-to-all-done.2
  563.7 3.1 reduce.4
  566.8 1.4 reshape.26
  568.2 1.0 copy.110
  569.3 2.9 convolution_bitcast_fusion
  573.5 9.8 %custom-call.19 = f32[1,128,128]{1,2,0:T(8,128)S(1)} custom-call(f32[1,128,128]{2,1,0:T(8,128)S(1)} %fusion.34), custom_call_target="InvertDiagBlocksLowerTriangular" | custom-call | tf_op jit(solution)/shard_map/jit(_solve_triangular)/triangular_solve | solution.py:12
  583.8 238.5 %all-reduce.5.cloned.1.call-done = f32[512,512]{1,0:T(8,128)} async-done(((f32[512,512]{1,0:T(8,128)}), f32[512,512]{1,0:T(8,128)}) %all-reduce.5.cloned.1.call-update) | async-done | bytes 1048592 | tf_op jit(solution)/shard_map/psum | solution.py:17
  822.2 2.3 fusion.76
  825.2 11.7 %cholesky.230 = f32[128,128]{1,0:T(8,128)S(1)} custom-call(f32[128,128]{1,0:T(8,128)S(1)} %fusion.46), custom_call_target="Cholesky" | custom-call | tf_op jit(solution)/shard_map/jit(cholesky)/cholesky | solution.py:11
  838.3 10.2 %custom-call.20 = f32[1,128,128]{1,2,0:T(8,128)S(1)} custom-call(f32[1,128,128]{2,1,0:T(8,128)S(1)} %fusion.35), custom_call_target="InvertDiagBlocksLowerTriangular" | custom-call | tf_op jit(solution)/shard_map/jit(_solve_triangular)/triangular_solve | solution.py:12
  848.9 2.2 fusion.78
  851.8 11.7 %cholesky.241 = f32[128,128]{1,0:T(8,128)S(1)} custom-call(f32[128,128]{1,0:T(8,128)S(1)} %fusion.44), custom_call_target="Cholesky" | custom-call | tf_op jit(solution)/shard_map/jit(cholesky)/cholesky | solution.py:11
  864.9 9.8 %custom-call.21 = f32[1,128,128]{1,2,0:T(8,128)S(1)} custom-call(f32[1,128,128]{2,1,0:T(8,128)S(1)} %fusion.36), custom_call_target="InvertDiagBlocksLowerTriangular" | custom-call | tf_op jit(solution)/shard_map/jit(_solve_triangular)/triangular_solve | solution.py:12
  876.8 11.9 %cholesky.252 = f32[128,128]{1,0:T(8,128)S(1)} custom-call(f32[128,128]{1,0:T(8,128)S(1)} %fusion.42), custom_call_target="Cholesky" | custom-call | tf_op jit(solution)/shard_map/jit(cholesky)/cholesky | solution.py:11
  890.0 9.8 %custom-call.22 = f32[1,128,128]{1,2,0:T(8,128)S(1)} custom-call(f32[1,128,128]{2,1,0:T(8,128)S(1)} %fusion.37), custom_call_target="InvertDiagBlocksLowerTriangular" | custom-call | tf_op jit(solution)/shard_map/jit(_solve_triangular)/triangular_solve | solution.py:12
  902.0 11.7 %cholesky.263 = f32[128,128]{1,0:T(8,128)S(1)} custom-call(f32[128,128]{1,0:T(8,128)S(1)} %fusion.40), custom_call_target="Cholesky" | custom-call | tf_op jit(solution)/shard_map/jit(cholesky)/cholesky | solution.py:11
  915.0 10.0 %custom-call.23 = f32[1,128,128]{1,2,0:T(8,128)S(1)} custom-call(f32[1,128,128]{2,1,0:T(8,128)S(1)} %fusion.38), custom_call_target="InvertDiagBlocksLowerTriangular" | custom-call | tf_op jit(solution)/shard_map/jit(_solve_triangular)/triangular_solve | solution.py:12
  925.5 1.8 convolution_bitcast_fusion.1
  928.1 6.4 all-to-all-start.3
  936.1 4.8 all-to-all-done.3
  (96 shorter events, 32.8 us)
Async XLA Ops:
  13.8 12.5 %copy-start.3 = (s32[512,128]{1,0:T(8,128)S(1)}, s32[512,128]{1,0:T(8,128)}, u32[]{:S(2)}) copy-start(s32[512,128]{1,0:T(8,128)} %param.7) | copy-start | bytes 786436
  13.8 105.2 %all-to-all-start = ((f32[16,64,1024]{2,0,1:T(8,128)}), f32[16,64,1024]{2,0,1:T(8,128)}, u32[]{:S(2)}, u32[]{:S(2)}) async-start(f32[16,64,1024]{2,0,1:T(8,128)} %copy.84), calls=%async_computation | async-start | bytes 8388608 | tf_op jit(solution)/shard_map/all_to_all | solution.py:24
  25.9 365.6 %all-reduce.3.cloned.1.call-start = ((), (), s32[]{:S(2)}) async-start(), calls=%async_computation.4 | async-start | bytes 2097152 | tf_op jit(solution)/shard_map/psum | solution.py:17
  126.4 1.9 copy-start
  391.5 52.7 %copy-start.1 = (f32[512,512]{1,0:T(8,128)S(1)}, f32[512,512]{1,0:T(8,128)}, u32[]{:S(2)}) copy-start(f32[512,512]{1,0:T(8,128)} %all-reduce.3.cloned.1.call-done) | copy-start | bytes 3145732
  539.0 9.0 copy-start.4
  541.8 21.3 %all-to-all-start.2 = ((f32[8,1,32768]{2,1,0:T(1,128)}), f32[8,1,32768]{2,1,0:T(1,128)S(1)}, u32[]{:S(2)}, u32[]{:S(2)}) async-start(f32[8,1,32768]{2,1,0:T(1,128)} %reshape.25), calls=%async_computation.2 | async-start | bytes 2097152 | tf_op jit(solution)/shard_map/all_to_all | solution.py:32
  548.1 274.2 %all-reduce.5.cloned.1.call-start = ((), (), s32[]{:S(2)}) async-start(), calls=%async_computation.5 | async-start | bytes 2097152 | tf_op jit(solution)/shard_map/psum | solution.py:17
  569.3 14.1 %copy-start.5 = (s32[512,128]{1,0:T(8,128)S(1)}, s32[512,128]{1,0:T(8,128)}, u32[]{:S(2)}) copy-start(s32[512,128]{1,0:T(8,128)} %param.8) | copy-start | bytes 786436
  822.2 52.9 %copy-start.2 = (f32[512,512]{1,0:T(8,128)S(1)}, f32[512,512]{1,0:T(8,128)}, u32[]{:S(2)}) copy-start(f32[512,512]{1,0:T(8,128)} %all-reduce.5.cloned.1.call-done) | copy-start | bytes 3145732
  928.1 12.9 %all-to-all-start.3 = ((f32[4,128,128]{2,0,1:T(4,128)}), f32[4,128,128]{2,0,1:T(4,128)S(1)}, u32[]{:S(2)}, u32[]{:S(2)}) async-start(f32[4,128,128]{2,0,1:T(4,128)} %copy.103), calls=%async_computation.3 | async-start | bytes 524288 | tf_op jit(solution)/shard_map/all_to_all | solution.py:46
Sparse Core Ops, SparseCore 0:
  136.9 254.5 all-reduce.2
  572.3 249.8 all-reduce.4
where the time goes:
time: 952 us; the launch traced here: 949 us
  waiting for transfers between devices  564 us (59%)
  other arithmetic  233 us (24%)
  matrix products  43 us (5%)
  blocking collectives  35.5 us (4%)
  local copies, waits for them, and re-layouts  33.7 us (4%)
  starting transfers between devices  25.1 us (3%)
  between operations  14.9 us (2%)
    psum x2, waiting for transfers between devices, leading_basis(): gram = lax.psum(partial_gram, ('px', 'py'))  476 us
    another operation x30, other arithmetic, orthonormal(): factor = jnp.linalg.cholesky(inner)  124 us
    another operation x20, other arithmetic, orthonormal(): return jax.scipy.linalg.solve_triangular(factor, matrix.T, lower=True).T  105 us
    all_to_all x1, waiting for transfers between devices, local(): lax.all_to_all(field, 'px', split_axis=1, concat_axis=0, tiled=True)  80.2 us
    all_to_all x1, blocking collectives, local(): lax.all_to_all(reduced, 'px', split_axis=0, concat_axis=1, tiled=True)  35.5 us
  transfers between devices with their start and end apart: 5, of which 5 were waited for; matrix products, arithmetic and copies ran while one was open for 6% of the time, Pallas kernels for 0%

commit v1 on v0

v1 whole, which is shorter than its diff:
```python
import jax
import jax.numpy as jnp
from jax import lax
from jax.sharding import Mesh, PartitionSpec as P

ITERS = 4
HI = lax.Precision.HIGHEST


def orthonormal(matrix):
    inner = jnp.dot(matrix.T, matrix, precision=HI)
    factor = jnp.linalg.cholesky(inner)
    return jax.scipy.linalg.solve_triangular(factor, matrix.T, lower=True).T


def total_gram(partial):
    tiles = partial.reshape(64, 8, 4, 128).transpose(0, 2, 1, 3).reshape(8, 32, 8, 128)
    got = lax.all_to_all(tiles, ("y", "c"), 0, 0, tiled=True)
    mine = jnp.sum(got, axis=0)
    got = lax.all_to_all(mine, ("z", "x"), 0, 0, tiled=True)
    one = jnp.sum(got, axis=0, keepdims=True)
    row = lax.all_to_all(jnp.broadcast_to(one, (32, 8, 128)), ("z", "x"), 0, 0, tiled=True)
    whole = lax.all_to_all(
        jnp.broadcast_to(row[None], (8, 32, 8, 128)), ("y", "c"), 0, 0, tiled=True
    )
    return whole.reshape(64, 4, 8, 128).transpose(0, 2, 1, 3).reshape(512, 512)


def leading_basis(gram, basis):
    for sweep in range(ITERS):
        basis = orthonormal(jnp.dot(gram, basis, precision=HI))
    return basis


def local(field, seeds_first, seeds_second):
    sent = field.reshape(16, 4, 16, 8, 128).transpose(3, 1, 0, 2, 4).reshape(32, 16, 16, 128)
    fibers = lax.all_to_all(sent, ("z", "x"), 0, 0, tiled=True)
    start_first = orthonormal(seeds_first.astype(jnp.float32))
    start_second = orthonormal(seeds_second.astype(jnp.float32))
    flat = fibers.reshape(512, 2048)
    partial_first = jnp.dot(flat, flat.T, precision=HI)
    basis_first = leading_basis(total_gram(partial_first), start_first)
    reduced = jnp.dot(basis_first.T, flat, precision=HI)
    slab = lax.all_to_all(reduced.reshape(32, 4, 16, 128), ("y", "c", "x"), 0, 0, tiled=True)
    turned = slab.transpose(0, 2, 1, 3).reshape(512, 512)
    partial_second = jnp.dot(turned, turned.T, precision=HI)
    basis_second = leading_basis(total_gram(partial_second), start_second)
    core = jnp.dot(basis_second.T, turned, precision=HI).reshape(8, 16, 4, 128)
    core = lax.all_to_all(core, ("y", "c"), 0, 0, tiled=True)
    core = lax.all_to_all(core, "z", 0, 0, tiled=True)
    core = core.transpose(2, 1, 0, 3).reshape(4, 16, 1024)
    return (basis_first, basis_second, core)


def solution(mesh):
    fine = Mesh(mesh.devices.reshape(8, 4, 4, 2), ("z", "x", "y", "c"))
    return jax.shard_map(
        local,
        mesh=fine,
        in_specs=(P(("z", "x"), ("y", "c"), None), P(), P()),
        out_specs=(P(), P(), P(("z", "x"), ("y", "c"), None)),
        check_vma=False,
    )
```

time: 952 us -> 570 us (0.60)
  waiting for transfers between devices: 564 us -> 25.8 us
  blocking collectives: 35.5 us -> 207 us
  between operations: 14.9 us -> 1.5 us
    psum x2 -> x0, waiting for transfers between devices: 476 us -> none  [leading_basis(): gram = lax.psum(partial_gram, ('px', 'py'))]
    all_to_all x1 -> x7, blocking collectives: 35.5 us -> 207 us  [the longest x1 105 us: local(): fibers = lax.all_to_all(sent, ('z', 'x'), 0, 0, tiled=True)]
    all_to_all x3 -> x5, waiting for transfers between devices: 87.7 us -> 25.8 us  [the longest x2 17.4 us: total_gram(): lax.all_to_all(jnp.broadcast_to(one, (32, 8, 128)), ('z', 'x'), 0, 0, til...]
    all_to_all x3 -> x5, starting transfers between devices: 24.7 us -> 25.6 us  [the longest x2 14.5 us: total_gram(): lax.all_to_all(jnp.broadcast_to(row[None], (8, 32, 8, 128)), ('y', 'c'),...]
  transfers between devices with their start and end apart: 5 -> 5, of which waited for: 5 -> 3; matrix products, arithmetic and copies ran while one was open for 6% -> 11% of each run, Pallas kernels for 0% -> 0%
where the time goes in v1:
time: 570 us; the launch traced here: 563 us
  other arithmetic  229 us (40%)
  blocking collectives  207 us (36%)
  matrix products  38.9 us (7%)
  local copies, waits for them, and re-layouts  34.9 us (6%)
  waiting for transfers between devices  25.8 us (5%)
  starting transfers between devices  25.6 us (4%)
    another operation x30, other arithmetic, orthonormal(): factor = jnp.linalg.cholesky(inner)  124 us
    all_to_all x1, blocking collectives, local(): fibers = lax.all_to_all(sent, ('z', 'x'), 0, 0, tiled=True)  105 us
    another operation x20, other arithmetic, orthonormal(): return jax.scipy.linalg.solve_triangular(factor, matrix.T, lower=True).T  105 us
    all_to_all x2, blocking collectives, total_gram(): got = lax.all_to_all(tiles, ('y', 'c'), 0, 0, tiled=True)  41.8 us
    all_to_all x2, blocking collectives, total_gram(): got = lax.all_to_all(mine, ('z', 'x'), 0, 0, tiled=True)  26.8 us
    all_to_all x1, blocking collectives, local(): lax.all_to_all(reduced.reshape(32, 4, 16, 128), ('y', 'c', 'x'), 0, 0, ti...  21.6 us
    all_to_all x2, waiting for transfers between devices, total_gram(): lax.all_to_all(jnp.broadcast_to(one, (32, 8, 128)), ('z', 'x'), 0, 0, til...  17.4 us
    all_to_all x2, starting transfers between devices, total_gram(): lax.all_to_all(jnp.broadcast_to(row[None], (8, 32, 8, 128)), ('y', 'c'),...  14.5 us
  transfers between devices with their start and end apart: 5, of which 3 were waited for; matrix products, arithmetic and copies ran while one was open for 11% of the time, Pallas kernels for 0%

profile of v1, /device:TPU:1, one launch (start us, length us, event | category | flops | bytes accessed | tf_op | source)
XLA Modules:
  0.0 562.8 jit_solution(11485903521285087912)
XLA Ops:
  0.6 3.2 copy.90
  4.6 105.4 %all_to_all.60 = f32[32,16,16,128]{3,2,1,0:T(8,128)} all-to-all(f32[32,16,16,128]{3,2,1,0:T(8,128)S(1)} %bitcast.236), channel_id=1, replica_groups=mesh['z'=8,'x'=4,'y'=4,'c'=2] {'z','x'}, dimensions={0} | all-to-all | bytes 8388608 | tf_op jit(solution)/shard_map/all_to_all | solution.py:37
  110.0 4.9 reshape.78
  114.9 4.9 reshape.79
  119.8 9.3 %fusion = f32[64,8,4,128]{3,1,2,0:T(8,128)S(1)} fusion(f32[4,128,2048,1]{2,1,0,3:T(8,128)} %reshape.79, f32[64,8,2048,1]{2,1,0,3:T(8,128)} %reshape.78), kind=kOutput, calls=%fused_computation.1 | convolution fusion | flops 6442450944 | bytes 9437184 | tf_op jit(solution)/shard_map/dot_general | solution.py:41
  129.2 22.3 %all_to_all.61 = f32[8,32,8,128]{3,2,1,0:T(8,128)S(1)} all-to-all(f32[8,32,8,128]{3,2,1,0:T(8,128)S(1)} %bitcast.240), channel_id=1, replica_groups=mesh['z'=8,'x'=4,'y'=4,'c'=2] {'y','c'}, dimensions={0} | all-to-all | bytes 2097152 | tf_op jit(solution)/shard_map/all_to_all | solution.py:18
  151.5 14.4 %all_to_all.62 = f32[32,8,128]{2,1,0:T(8,128)S(1)} all-to-all(f32[32,8,128]{2,1,0:T(8,128)S(1)} %reduce_sum.36), channel_id=1, replica_groups=mesh['z'=8,'x'=4,'y'=4,'c'=2] {'z','x'}, dimensions={0} | all-to-all | bytes 262144 | tf_op jit(solution)/shard_map/all_to_all | solution.py:20
  166.7 3.9 all-to-all-start.3
  171.2 8.7 %all-to-all-done.3 = f32[32,8,128]{2,1,0:T(8,128)S(1)} async-done(((f32[32,8,128]{2,1,0:T(8,128)}), f32[32,8,128]{2,1,0:T(8,128)S(1)}, u32[]{:S(2)}, u32[]{:S(2)}) %all-to-all-start.3) | async-done | bytes 131104 | tf_op jit(solution)/shard_map/all_to_all | solution.py:22
  179.9 1.1 broadcast_in_dim.10
  181.1 7.4 %all-to-all-start.4 = ((f32[8,32,8,128]{3,2,1,0:T(8,128)}), f32[8,32,8,128]{3,2,1,0:T(8,128)S(1)}, u32[]{:S(2)}, u32[]{:S(2)}) async-start(f32[8,32,8,128]{3,2,1,0:T(8,128)} %broadcast_in_dim.10), calls=%async_computation.4 | async-start | bytes 2097152 | tf_op jit(solution)/shard_map/all_to_all | solution.py:23
  188.5 11.7 %cholesky.164 = f32[128,128]{1,0:T(8,128)S(1)} custom-call(f32[128,128]{1,0:T(8,128)S(1)} %fusion.61), custom_call_target="Cholesky" | custom-call | tf_op jit(solution)/shard_map/jit(cholesky)/cholesky | solution.py:12
  201.6 9.8 %custom-call.14 = f32[1,128,128]{1,2,0:T(8,128)S(1)} custom-call(f32[1,128,128]{2,1,0:T(8,128)S(1)} %fusion.32), custom_call_target="InvertDiagBlocksLowerTriangular" | custom-call | tf_op jit(solution)/shard_map/jit(_solve_triangular)/triangular_solve | solution.py:13
  211.8 6.1 %copy.98 = f32[64,8,16,128]{3,1,2,0:T(8,128)} copy(f32[64,8,16,128]{3,2,1,0:T(8,128)} %bitcast.226) | data formatting | bytes 8388608
  217.9 5.8 %copy.68 = f32[512,2048]{0,1:T(8,128)} copy(f32[512,2048]{1,0:T(8,128)} %bitcast.237) | data formatting | bytes 8388608 | tf_op jit(solution)/shard_map/reshape | solution.py:40
  225.5 11.7 %cholesky.175 = f32[128,128]{1,0:T(8,128)S(1)} custom-call(f32[128,128]{1,0:T(8,128)S(1)} %fusion.59), custom_call_target="Cholesky" | custom-call | tf_op jit(solution)/shard_map/jit(cholesky)/cholesky | solution.py:12
  238.6 9.8 %custom-call.15 = f32[1,128,128]{1,2,0:T(8,128)S(1)} custom-call(f32[1,128,128]{2,1,0:T(8,128)S(1)} %fusion.33), custom_call_target="InvertDiagBlocksLowerTriangular" | custom-call | tf_op jit(solution)/shard_map/jit(_solve_triangular)/triangular_solve | solution.py:13
  250.5 11.9 %cholesky.186 = f32[128,128]{1,0:T(8,128)S(1)} custom-call(f32[128,128]{1,0:T(8,128)S(1)} %fusion.57), custom_call_target="Cholesky" | custom-call | tf_op jit(solution)/shard_map/jit(cholesky)/cholesky | solution.py:12
  263.7 9.8 %custom-call.16 = f32[1,128,128]{1,2,0:T(8,128)S(1)} custom-call(f32[1,128,128]{2,1,0:T(8,128)S(1)} %fusion.34), custom_call_target="InvertDiagBlocksLowerTriangular" | custom-call | tf_op jit(solution)/shard_map/jit(_solve_triangular)/triangular_solve | solution.py:13
  275.6 11.7 %cholesky.197 = f32[128,128]{1,0:T(8,128)S(1)} custom-call(f32[128,128]{1,0:T(8,128)S(1)} %fusion.55), custom_call_target="Cholesky" | custom-call | tf_op jit(solution)/shard_map/jit(cholesky)/cholesky | solution.py:12
  288.7 9.8 %custom-call.17 = f32[1,128,128]{1,2,0:T(8,128)S(1)} custom-call(f32[1,128,128]{2,1,0:T(8,128)S(1)} %fusion.35), custom_call_target="InvertDiagBlocksLowerTriangular" | custom-call | tf_op jit(solution)/shard_map/jit(_solve_triangular)/triangular_solve | solution.py:13
  298.9 1.4 fusion.76
  301.0 11.7 %cholesky.208 = f32[128,128]{1,0:T(8,128)S(1)} custom-call(f32[128,128]{1,0:T(8,128)S(1)} %fusion.53), custom_call_target="Cholesky" | custom-call | tf_op jit(solution)/shard_map/jit(cholesky)/cholesky | solution.py:12
  314.1 9.8 %custom-call.18 = f32[1,128,128]{1,2,0:T(8,128)S(1)} custom-call(f32[1,128,128]{2,1,0:T(8,128)S(1)} %fusion.36), custom_call_target="InvertDiagBlocksLowerTriangular" | custom-call | tf_op jit(solution)/shard_map/jit(_solve_triangular)/triangular_solve | solution.py:13
  324.4 6.1 %fusion.14 = f32[32,4,16,128]{3,0,2,1:T(8,128)S(1)} fusion(f32[16,128,512,1]{2,1,0,3:T(8,128)} %bitcast.235, f32[32,4,512,1]{2,1,0,3:T(4,128)S(1)} %bitcast.249), kind=kOutput, calls=%fused_computation.17 | convolution fusion | flops 1610612736 | bytes 5505024 | tf_op jit(solution)/shard_map/dot_general | solution.py:43
  331.1 21.6 %all_to_all.63 = f32[32,4,16,128]{3,2,1,0:T(8,128)S(1)} all-to-all(f32[32,4,16,128]{3,2,1,0:T(8,128)S(1)} %copy.70), channel_id=1, replica_groups=mesh['z'=8,'x'=4,'y'=4,'c'=2] {'y','c','x'}, dimensions={0} | all-to-all | bytes 2097152 | tf_op jit(solution)/shard_map/all_to_all | solution.py:44
  354.0 1.9 fusion.2
  355.9 19.5 %all_to_all.64 = f32[8,32,8,128]{3,2,1,0:T(8,128)S(1)} all-to-all(f32[8,32,8,128]{3,2,1,0:T(8,128)S(1)} %bitcast.241), channel_id=1, replica_groups=mesh['z'=8,'x'=4,'y'=4,'c'=2] {'y','c'}, dimensions={0} | all-to-all | bytes 2097152 | tf_op jit(solution)/shard_map/all_to_all | solution.py:18
  375.4 12.4 %all_to_all.65 = f32[32,8,128]{2,1,0:T(8,128)S(1)} all-to-all(f32[32,8,128]{2,1,0:T(8,128)S(1)} %reduce_sum.38), channel_id=1, replica_groups=mesh['z'=8,'x'=4,'y'=4,'c'=2] {'z','x'}, dimensions={0} | all-to-all | bytes 262144 | tf_op jit(solution)/shard_map/all_to_all | solution.py:20
  388.5 3.9 all-to-all-start.8
  393.1 8.7 %all-to-all-done.8 = f32[32,8,128]{2,1,0:T(8,128)S(1)} async-done(((f32[32,8,128]{2,1,0:T(8,128)}), f32[32,8,128]{2,1,0:T(8,128)S(1)}, u32[]{:S(2)}, u32[]{:S(2)}) %all-to-all-start.8) | async-done | bytes 131104 | tf_op jit(solution)/shard_map/all_to_all | solution.py:22
  402.8 7.1 %all-to-all-start.9 = ((f32[8,32,8,128]{3,2,1,0:T(8,128)}), f32[8,32,8,128]{3,2,1,0:T(8,128)S(1)}, u32[]{:S(2)}, u32[]{:S(2)}) async-start(f32[8,32,8,128]{3,2,1,0:T(8,128)} %broadcast_in_dim.12), calls=%async_computation.9 | async-start | bytes 2097152 | tf_op jit(solution)/shard_map/all_to_all | solution.py:23
  409.9 11.7 %cholesky.219 = f32[128,128]{1,0:T(8,128)S(1)} custom-call(f32[128,128]{1,0:T(8,128)S(1)} %fusion.51), custom_call_target="Cholesky" | custom-call | tf_op jit(solution)/shard_map/jit(cholesky)/cholesky | solution.py:12
  423.0 9.8 %custom-call.19 = f32[1,128,128]{1,2,0:T(8,128)S(1)} custom-call(f32[1,128,128]{2,1,0:T(8,128)S(1)} %fusion.37), custom_call_target="InvertDiagBlocksLowerTriangular" | custom-call | tf_op jit(solution)/shard_map/jit(_solve_triangular)/triangular_solve | solution.py:13
  432.8 1.1 fusion.12
  434.3 1.9 fusion.78
  437.0 11.8 %cholesky.230 = f32[128,128]{1,0:T(8,128)S(1)} custom-call(f32[128,128]{1,0:T(8,128)S(1)} %fusion.49), custom_call_target="Cholesky" | custom-call | tf_op jit(solution)/shard_map/jit(cholesky)/cholesky | solution.py:12
  450.1 9.8 %custom-call.20 = f32[1,128,128]{1,2,0:T(8,128)S(1)} custom-call(f32[1,128,128]{2,1,0:T(8,128)S(1)} %fusion.38), custom_call_target="InvertDiagBlocksLowerTriangular" | custom-call | tf_op jit(solution)/shard_map/jit(_solve_triangular)/triangular_solve | solution.py:13
  462.1 11.7 %cholesky.241 = f32[128,128]{1,0:T(8,128)S(1)} custom-call(f32[128,128]{1,0:T(8,128)S(1)} %fusion.47), custom_call_target="Cholesky" | custom-call | tf_op jit(solution)/shard_map/jit(cholesky)/cholesky | solution.py:12
  475.1 9.8 %custom-call.21 = f32[1,128,128]{1,2,0:T(8,128)S(1)} custom-call(f32[1,128,128]{2,1,0:T(8,128)S(1)} %fusion.39), custom_call_target="InvertDiagBlocksLowerTriangular" | custom-call | tf_op jit(solution)/shard_map/jit(_solve_triangular)/triangular_solve | solution.py:13
  487.5 11.7 %cholesky.252 = f32[128,128]{1,0:T(8,128)S(1)} custom-call(f32[128,128]{1,0:T(8,128)S(1)} %fusion.45), custom_call_target="Cholesky" | custom-call | tf_op jit(solution)/shard_map/jit(cholesky)/cholesky | solution.py:12
  500.5 9.8 %custom-call.22 = f32[1,128,128]{1,2,0:T(8,128)S(1)} custom-call(f32[1,128,128]{2,1,0:T(8,128)S(1)} %fusion.40), custom_call_target="InvertDiagBlocksLowerTriangular" | custom-call | tf_op jit(solution)/shard_map/jit(_solve_triangular)/triangular_solve | solution.py:13
  512.5 11.7 %cholesky.263 = f32[128,128]{1,0:T(8,128)S(1)} custom-call(f32[128,128]{1,0:T(8,128)S(1)} %fusion.43), custom_call_target="Cholesky" | custom-call | tf_op jit(solution)/shard_map/jit(cholesky)/cholesky | solution.py:12
  525.7 9.8 %custom-call.23 = f32[1,128,128]{1,2,0:T(8,128)S(1)} custom-call(f32[1,128,128]{2,1,0:T(8,128)S(1)} %fusion.41), custom_call_target="InvertDiagBlocksLowerTriangular" | custom-call | tf_op jit(solution)/shard_map/jit(_solve_triangular)/triangular_solve | solution.py:13
  535.9 1.2 fusion.86
  537.1 11.2 %all_to_all.66 = f32[8,16,4,128]{3,1,2,0:T(8,128)} all-to-all(f32[8,16,4,128]{3,1,2,0:T(8,128)S(1)} %fusion.86), channel_id=1, replica_groups=mesh['z'=8,'x'=4,'y'=4,'c'=2] {'y','c'}, dimensions={0} | all-to-all | bytes 524288 | tf_op jit(solution)/shard_map/all_to_all | solution.py:49
  548.4 3.4 all-to-all-start.11
  553.4 8.4 %all-to-all-done.11 = f32[8,16,4,128]{3,1,2,0:T(8,128)S(1)} async-done(((f32[8,16,4,128]{3,1,2,0:T(8,128)}), f32[8,16,4,128]{3,1,2,0:T(8,128)S(1)}, u32[]{:S(2)}, u32[]{:S(2)}) %all-to-all-start.11) | async-done | bytes 262176 | tf_op jit(solution)/shard_map/all_to_all | solution.py:50
  (99 shorter events, 38.6 us)
Async XLA Ops:
  129.2 41.4 %copy-start = (s32[512,128]{1,0:T(8,128)S(1)}, s32[512,128]{1,0:T(8,128)}, u32[]{:S(2)}) copy-start(s32[512,128]{1,0:T(8,128)} %param.7) | copy-start | bytes 786436
  166.7 13.3 %all-to-all-start.3 = ((f32[32,8,128]{2,1,0:T(8,128)}), f32[32,8,128]{2,1,0:T(8,128)S(1)}, u32[]{:S(2)}, u32[]{:S(2)}) async-start(f32[32,8,128]{2,1,0:T(8,128)} %broadcast_in_dim.9), calls=%async_computation.3 | async-start | bytes 262144 | tf_op jit(solution)/shard_map/all_to_all | solution.py:22
  181.1 42.7 %all-to-all-start.4 = ((f32[8,32,8,128]{3,2,1,0:T(8,128)}), f32[8,32,8,128]{3,2,1,0:T(8,128)S(1)}, u32[]{:S(2)}, u32[]{:S(2)}) async-start(f32[8,32,8,128]{3,2,1,0:T(8,128)} %broadcast_in_dim.10), calls=%async_computation.4 | async-start | bytes 2097152 | tf_op jit(solution)/shard_map/all_to_all | solution.py:23
  355.9 36.5 %copy-start.1 = (s32[512,128]{1,0:T(8,128)S(1)}, s32[512,128]{1,0:T(8,128)}, u32[]{:S(2)}) copy-start(s32[512,128]{1,0:T(8,128)} %param.8) | copy-start | bytes 786436
  388.5 13.3 %all-to-all-start.8 = ((f32[32,8,128]{2,1,0:T(8,128)}), f32[32,8,128]{2,1,0:T(8,128)S(1)}, u32[]{:S(2)}, u32[]{:S(2)}) async-start(f32[32,8,128]{2,1,0:T(8,128)} %broadcast_in_dim.11), calls=%async_computation.8 | async-start | bytes 262144 | tf_op jit(solution)/shard_map/all_to_all | solution.py:22
  402.8 31.5 %all-to-all-start.9 = ((f32[8,32,8,128]{3,2,1,0:T(8,128)}), f32[8,32,8,128]{3,2,1,0:T(8,128)S(1)}, u32[]{:S(2)}, u32[]{:S(2)}) async-start(f32[8,32,8,128]{3,2,1,0:T(8,128)} %broadcast_in_dim.12), calls=%async_computation.9 | async-start | bytes 2097152 | tf_op jit(solution)/shard_map/all_to_all | solution.py:23
  548.4 13.5 %all-to-all-start.11 = ((f32[8,16,4,128]{3,1,2,0:T(8,128)}), f32[8,16,4,128]{3,1,2,0:T(8,128)S(1)}, u32[]{:S(2)}, u32[]{:S(2)}) async-start(f32[8,16,4,128]{3,1,2,0:T(8,128)} %all_to_all.66), calls=%async_computation.11 | async-start | bytes 524288 | tf_op jit(solution)/shard_map/all_to_all | solution.py:50

commit v2 on v1

v2 whole, which is shorter than its diff:
```python
import jax
import jax.numpy as jnp
from jax import lax
from jax.experimental import pallas as pl
from jax.experimental.pallas import tpu as pltpu
from jax.sharding import Mesh, PartitionSpec as P

ITERS = 4
N = 512
RANK = 128
F32 = jnp.float32
BF16 = jnp.bfloat16
NN = (((1,), (0,)), ((), ()))
NT = (((1,), (1,)), ((), ()))
TILES = [(row, col) for row in range(64) for col in range(row // 16, 4)]
HALF = len(TILES) // 2
PARAMS = pltpu.CompilerParams(vmem_limit_bytes=56 * 2**20)
VMEM = pl.BlockSpec(memory_space=pltpu.VMEM)
SMEM = pl.BlockSpec(memory_space=pltpu.SMEM)
ANY = pl.BlockSpec(memory_space=pl.ANY)


def dot(left, right, dims):
    return lax.dot_general(left, right, dims, preferred_element_type=F32)


def split(x):
    high = x.astype(BF16)
    return high, (x - high.astype(F32)).astype(BF16)


def as_left(x):
    high, low = split(x)
    return jnp.concatenate([high, low, high], axis=1)


def as_right_rows(x):
    high, low = split(x)
    return jnp.concatenate([high, high, low], axis=0)


def as_right_cols(x):
    high, low = split(x)
    return jnp.concatenate([high, high, low], axis=1)


def inverse_factor(inner):
    sub = lax.broadcasted_iota(jnp.int32, (8, RANK), 0)
    lane = lax.broadcasted_iota(jnp.int32, (8, RANK), 1)
    panels = RANK // 8
    left = [inner[8 * i : 8 * i + 8, :] for i in range(panels)]
    right = [jnp.where(lane == sub + 8 * i, 1.0, 0.0).astype(F32) for i in range(panels)]
    spread = lambda row: jnp.broadcast_to(row, (8, RANK))
    out = []
    for p in range(panels):
        rows = range(p, panels)
        cols = {i: [spread(left[i][:, 8 * p + t : 8 * p + t + 1]) for t in range(8)] for i in rows}
        done = jnp.zeros((8, RANK), F32)
        for t in range(8):
            root = lax.rsqrt(spread(cols[p][t][t : t + 1, :]))
            left_row = spread(left[p][t : t + 1, :]) * root
            right_row = spread(right[p][t : t + 1, :]) * root
            done = jnp.where(sub == t, right_row, done)
            ahead = [spread(cols[p][u][t : t + 1, :]) * root for u in range(t + 1, 8)]
            for i in rows:
                factor = cols[i][t] * root
                left[i] = left[i] - factor * left_row
                right[i] = right[i] - factor * right_row
                for k, u in enumerate(range(t + 1, 8)):
                    cols[i][u] = cols[i][u] - factor * ahead[k]
        out.append(done)
    return jnp.concatenate(out, axis=0)


def orthonormal(turned):
    inner = dot(as_left(turned), as_right_cols(turned), NT)
    return dot(as_left(inverse_factor(inner)), as_right_rows(turned), NN)


def seeds_kernel(first_ref, second_ref, first_out, second_out):
    first_out[...] = orthonormal(first_ref[...].astype(F32))
    second_out[...] = orthonormal(second_ref[...].astype(F32))


def upper_gram(high, low, mine_ref, other_ref, swap, core):
    for block in range(4):
        rows = slice(128 * block, 128 * block + 128)
        cols = slice(128 * block, N)
        gram = dot(
            jnp.concatenate([high[rows, :], low[rows, :], high[rows, :]], axis=1),
            jnp.concatenate([high[cols, :], high[cols, :], low[cols, :]], axis=1),
            NT,
        )
        for at, (row, col) in enumerate(TILES):
            if row // 16 == block:
                r, c = 8 * (row % 16), 128 * (col - block)
                half = lax.bitwise_xor(at // HALF, core)
                swap[half, at % HALF] = gram[r : r + 8, c : c + 128]
    mine_ref[...] = swap[0]
    other_ref[...] = swap[1]


def first_gram_kernel(core_ref, fibers_ref, mine_ref, other_ref, high, low, swap):
    flat = fibers_ref.reshape(N * 16, 128)
    for j in range(16):
        h, l = split(flat[pl.ds(j, N, stride=16), :])
        high[:, 128 * j : 128 * j + 128] = h
        low[:, 128 * j : 128 * j + 128] = l
    upper_gram(high, low, mine_ref, other_ref, swap, core_ref[0])


def second_gram_kernel(core_ref, slab_ref, mine_ref, other_ref, high, low, swap):
    for a in range(4):
        h, l = split(slab_ref[:, a].reshape(N, 128))
        high[:, 128 * a : 128 * a + 128] = h
        low[:, 128 * a : 128 * a + 128] = l
    upper_gram(high, low, mine_ref, other_ref, swap, core_ref[0])


def leading(core_ref, mine_ref, other_ref, start_ref, whole, gram, parts):
    core = core_ref[0]
    whole[core] = mine_ref[...]
    whole[1 - core] = other_ref[...]
    for at, (row, col) in enumerate(TILES):
        gram[8 * row : 8 * row + 8, 128 * col : 128 * col + 128] = whole[at // HALF, at % HALF]
    for row in range(1, 4):
        for col in range(row):
            gram[128 * row : 128 * row + 128, 128 * col : 128 * col + 128] = gram[
                128 * col : 128 * col + 128, 128 * row : 128 * row + 128
            ].T
    parts[...] = as_right_rows(gram[...])

    def sweep(_, basis):
        return orthonormal(dot(as_left(basis), parts[...], NN))

    return lax.fori_loop(0, ITERS, sweep, start_ref[...])


def first_basis_kernel(
    core_ref, mine_ref, other_ref, start_ref, fibers_hbm, basis_ref, reduced_ref, whole, gram, parts, fibers, sem
):
    copy = pltpu.make_async_copy(fibers_hbm, fibers, sem)
    copy.start()
    basis = leading(core_ref, mine_ref, other_ref, start_ref, whole, gram, parts)
    basis_ref[...] = basis.T
    basis = as_left(basis)
    copy.wait()
    flat = fibers.reshape(N * 16, 128)
    out = reduced_ref.reshape(RANK * 16, 128)
    for j in range(0, 16, 2):
        pair = jnp.concatenate([flat[pl.ds(j, N, stride=16), :], flat[pl.ds(j + 1, N, stride=16), :]], axis=1)
        reduced = dot(basis, as_right_rows(pair), NN)
        out[pl.ds(j, RANK, stride=16), :] = reduced[:, :128]
        out[pl.ds(j + 1, RANK, stride=16), :] = reduced[:, 128:]


def second_basis_kernel(core_ref, mine_ref, other_ref, start_ref, slab_ref, basis_ref, core_out, whole, gram, parts):
    basis = leading(core_ref, mine_ref, other_ref, start_ref, whole, gram, parts)
    basis_ref[...] = basis.T
    basis = as_left(basis)
    for a in range(0, 4, 2):
        pair = jnp.concatenate([slab_ref[:, a].reshape(N, 128), slab_ref[:, a + 1].reshape(N, 128)], axis=1)
        got = dot(basis, as_right_rows(pair), NN)
        core_out[:, a] = got[:, :128].reshape(8, 16, 128)
        core_out[:, a + 1] = got[:, 128:].reshape(8, 16, 128)


def shaped(*shape):
    return jax.ShapeDtypeStruct(shape, F32)


def gram_call(kernel, depth, core, x):
    return pl.pallas_call(
        kernel,
        out_shape=(shaped(HALF, 8, 128), shaped(HALF, 8, 128)),
        in_specs=[SMEM, VMEM],
        out_specs=(VMEM, VMEM),
        scratch_shapes=[
            pltpu.VMEM((N, depth), BF16),
            pltpu.VMEM((N, depth), BF16),
            pltpu.VMEM((2, HALF, 8, 128), F32),
        ],
        compiler_params=PARAMS,
    )(core, x)


LEADING_SCRATCH = [
    pltpu.VMEM((2, HALF, 8, 128), F32),
    pltpu.VMEM((N, N), F32),
    pltpu.VMEM((3 * N, N), BF16),
]


def across_cores(x):
    return lax.ppermute(x, "c", [(0, 1), (1, 0)])


def total(mine, other):
    share = HALF // 16
    mine = (mine + across_cores(other)).reshape(16, share, 8, 128)
    got = jnp.sum(lax.all_to_all(mine, ("x", "y"), 0, 0, tiled=True), axis=0)
    got = jnp.sum(lax.all_to_all(jnp.broadcast_to(got, (8, share, 8, 128)), "z", 0, 0, tiled=True), axis=0)
    got = lax.all_to_all(jnp.broadcast_to(got, (16, share, 8, 128)), ("x", "y"), 0, 0, tiled=True)
    got = got.reshape(HALF, 8, 128)
    return got, across_cores(got)


def local(field, seeds_first, seeds_second):
    core = lax.axis_index("c").reshape(1)
    sent = field.reshape(16, 4, 16, 8, 128).transpose(3, 1, 0, 2, 4).reshape(32, 16, 16, 128)
    fibers = lax.all_to_all(sent, ("z", "x"), 0, 0, tiled=True).reshape(N, 16, 128)
    starts = pl.pallas_call(
        seeds_kernel, out_shape=(shaped(RANK, N), shaped(RANK, N)), compiler_params=PARAMS
    )(seeds_first.T, seeds_second.T)

    mine, other = total(*gram_call(first_gram_kernel, 2048, core, fibers))
    basis_first, reduced = pl.pallas_call(
        first_basis_kernel,
        out_shape=(shaped(N, RANK), shaped(RANK, 16, 128)),
        in_specs=[SMEM, VMEM, VMEM, VMEM, ANY],
        out_specs=(VMEM, VMEM),
        scratch_shapes=LEADING_SCRATCH + [pltpu.VMEM((N, 16, 128), F32), pltpu.SemaphoreType.DMA],
        compiler_params=PARAMS,
    )(core, mine, other, starts[0], fibers)

    slab = lax.all_to_all(reduced.reshape(32, 4, 16, 128), ("y", "c", "x"), 0, 0, tiled=True)
    mine, other = total(*gram_call(second_gram_kernel, 512, core, slab))
    basis_second, ranks = pl.pallas_call(
        second_basis_kernel,
        out_shape=(shaped(N, RANK), shaped(8, 4, 16, 128)),
        in_specs=[SMEM, VMEM, VMEM, VMEM, VMEM],
        out_specs=(VMEM, VMEM),
        scratch_shapes=LEADING_SCRATCH,
        compiler_params=PARAMS,
    )(core, mine, other, starts[1], slab)
    ranks = lax.all_to_all(ranks, ("y", "c"), 0, 0, tiled=True)
    ranks = lax.all_to_all(ranks, "z", 0, 0, tiled=True)
    core_tensor = ranks.transpose(1, 2, 0, 3).reshape(4, 16, 1024)
    return (basis_first, basis_second, core_tensor)


def solution(mesh):
    fine = Mesh(mesh.devices.reshape(8, 4, 4, 2), ("z", "x", "y", "c"))
    return jax.shard_map(
        local,
        mesh=fine,
        in_specs=(P(("z", "x"), ("y", "c"), None), P(), P()),
        out_specs=(P(), P(), P(("z", "x"), ("y", "c"), None)),
        check_vma=False,
    )
```

time: 570 us -> 320 us (0.56); the launches traced: 563 us -> 319 us
  other arithmetic: 229 us -> 2.12 us
  blocking collectives: 207 us -> 115 us
  waiting for transfers between devices: 25.8 us -> 97.2 us
  Pallas kernels: 0 us -> 70.3 us
  matrix products: 38.9 us -> 0 us
  local copies, waits for them, and re-layouts: 34.9 us -> 9.87 us
    another operation x50 -> x0, other arithmetic: 229 us -> none  [the longest x30 124 us: orthonormal(): factor = jnp.linalg.cholesky(inner)]
    all_to_all x6 -> x8, blocking collectives: 185 us -> 94.6 us  [the longest x2 27.2 us: total(): got = jnp.sum(lax.all_to_all(mine, ('x', 'y'), 0, 0, tiled=True), axis=0)]
    pallas_call x0 -> x5, Pallas kernels: none -> 70.3 us  [the longest x1 24.5 us: local(): pl.pallas_call(first_basis_kernel, out_shape=(shaped(N, RANK), shaped(RAN...]
    all_to_all x5 -> x1, waiting for transfers between devices: 25.8 us -> 93 us  [local(): lax.all_to_all(sent, ('z', 'x'), 0, 0, tiled=True).reshape(N, 16, 128)]
    dot_general x22 -> x0, matrix products: 34 us -> none  [the longest x1 9.34 us: local(): partial_first = jnp.dot(flat, flat.T, precision=HI)]
    all_to_all x5 -> x1, starting transfers between devices: 25.6 us -> 12 us  [local(): lax.all_to_all(sent, ('z', 'x'), 0, 0, tiled=True).reshape(N, 16, 128)]
    dot_general x17 -> x0, local copies, waits for them, and re-layouts: 12.5 us -> none  [the longest x2 9.79 us: local(): partial_first = jnp.dot(flat, flat.T, precision=HI)]
    ppermute x0 -> x4, starting transfers between devices: none -> 11.5 us  [across_cores(): return lax.ppermute(x, 'c', [(0, 1), (1, 0)])]
  transfers between devices with their start and end apart: 5 -> 5, of which waited for: 3 -> 4; matrix products, arithmetic and copies ran while one was open for 11% -> 1% of each run, Pallas kernels for 0% -> 3%
where the time goes in v2:
time: 320 us; the launch traced here: 319 us
  blocking collectives  115 us (36%)
  waiting for transfers between devices  97.2 us (30%)
  Pallas kernels  70.3 us (22%)
  starting transfers between devices  23.5 us (7%)
  local copies, waits for them, and re-layouts  9.87 us (3%)
    all_to_all x1, waiting for transfers between devices, local(): lax.all_to_all(sent, ('z', 'x'), 0, 0, tiled=True).reshape(N, 16, 128)  93 us
    all_to_all x2, blocking collectives, total(): got = jnp.sum(lax.all_to_all(mine, ('x', 'y'), 0, 0, tiled=True), axis=0)  27.2 us
    pallas_call x1, Pallas kernels, local(): pl.pallas_call(first_basis_kernel, out_shape=(shaped(N, RANK), shaped(RAN...  24.5 us
    all_to_all x2, blocking collectives, total(): lax.all_to_all(jnp.broadcast_to(got, (16, share, 8, 128)), ('x', 'y'), 0,...  23.2 us
    pallas_call x1, Pallas kernels, local(): pl.pallas_call(second_basis_kernel, out_shape=(shaped(N, RANK), shaped(8,...  22.3 us
    all_to_all x2, blocking collectives, total(): lax.all_to_all(jnp.broadcast_to(got, (8, share, 8, 128)), 'z', 0, 0, tile...  21.5 us
    all_to_all x1, blocking collectives, local(): lax.all_to_all(reduced.reshape(32, 4, 16, 128), ('y', 'c', 'x'), 0, 0, ti...  20.4 us
    pallas_call x2, Pallas kernels, gram_call(): pl.pallas_call(kernel, out_shape=(shaped(HALF, 8, 128), shaped(HALF, 8, 1...  12.7 us
  transfers between devices with their start and end apart: 5, of which 4 were waited for; matrix products, arithmetic and copies ran while one was open for 1% of the time, Pallas kernels for 3%

profile of v2, /device:TPU:1, one launch (start us, length us, event | category | flops | bytes accessed | tf_op | source)
XLA Modules:
  0.0 318.7 jit_solution(18344634557274999004)
XLA Ops:
  0.6 3.2 %copy.18 = f32[128,8,8,128]{3,2,1,0:T(8,128)S(1)} copy(f32[128,8,8,128]{3,1,2,0:T(8,128)} %bitcast.24) | data formatting | bytes 8388608
  3.8 2.7 copy.13
  6.6 12.0 %all-to-all-start = ((f32[32,16,16,128]{3,2,1,0:T(8,128)}), f32[32,16,16,128]{3,2,1,0:T(8,128)}, u32[]{:S(2)}, u32[]{:S(2)}) async-start(f32[32,16,16,128]{3,2,1,0:T(8,128)} %bitcast.22), calls=%async_computation | async-start | bytes 8388608 | tf_op jit(solution)/shard_map/all_to_all | solution.py:211
  18.6 0.0 copy-start.4
  18.6 93.0 %all-to-all-done = f32[32,16,16,128]{3,2,1,0:T(8,128)} async-done(((f32[32,16,16,128]{3,2,1,0:T(8,128)}), f32[32,16,16,128]{3,2,1,0:T(8,128)}, u32[]{:S(2)}, u32[]{:S(2)}) %all-to-all-start) | async-done | bytes 4194336 | tf_op jit(solution)/shard_map/all_to_all | solution.py:211
  111.6 0.0 copy-start.5
  111.6 9.2 %shard_map.58 = (f32[80,8,128]{2,1,0:T(8,128)}, f32[80,8,128]{2,1,0:T(8,128)}) custom-call(s32[1]{0:T(128)} %bitcast.core_ref, f32[512,16,128]{2,1,0:T(8,128)} %bitcast.3.fibers_ref.fibers_hbm), custom_call_target="tpu_custom_call" | custom-call | tf_op jit(solution)/shard_map/pallas_call | solution.py:173
  120.8 2.3 collective-permute-start
  123.1 1.5 collective-permute-done
  124.5 1.0 add.6
  125.5 15.8 %all_to_all.50 = f32[16,5,8,128]{3,2,1,0:T(8,128)S(1)} all-to-all(f32[16,5,8,128]{3,2,1,0:T(8,128)S(1)} %bitcast.27), channel_id=1, replica_groups=mesh['z'=8,'x'=4,'y'=4,'c'=2] {'x','y'}, dimensions={0} | all-to-all | bytes 655360 | tf_op jit(solution)/shard_map/all_to_all | solution.py:201
  141.4 10.8 %all_to_all.51 = f32[8,5,8,128]{3,2,1,0:T(8,128)S(1)} all-to-all(f32[8,5,8,128]{3,2,1,0:T(8,128)S(1)} %broadcast_in_dim.12), channel_id=1, replica_groups=mesh['z'=8,'x'=4,'y'=4,'c'=2] {'z'}, dimensions={0} | all-to-all | bytes 327680 | tf_op jit(solution)/shard_map/all_to_all | solution.py:202
  152.2 11.6 %all_to_all.52 = f32[16,5,8,128]{3,2,1,0:T(8,128)S(1)} all-to-all(f32[16,5,8,128]{3,2,1,0:T(8,128)S(1)} %broadcast_in_dim.13), channel_id=1, replica_groups=mesh['z'=8,'x'=4,'y'=4,'c'=2] {'x','y'}, dimensions={0} | all-to-all | bytes 655360 | tf_op jit(solution)/shard_map/all_to_all | solution.py:203
  163.8 0.0 copy-start.1
  163.8 4.0 %collective-permute-start.1 = (f32[80,8,128]{2,1,0:T(8,128)S(1)}, f32[80,8,128]{2,1,0:T(8,128)S(1)}, u32[]{:S(2)}, u32[]{:S(2)}) collective-permute-start(f32[80,8,128]{2,1,0:T(8,128)S(1)} %bitcast.29), channel_id=1, source_target_pairs={{0,1},{1,0},{2,3},{3,2},{4,5},{5,4},{6,7},{7,6},{8,9},{9,8},{10,11... | collective-permute-start | bytes 983048 | tf_op jit(solution)/shard_map/ppermute | solution.py:195
  167.8 0.0 copy-done.4
  167.8 0.8 copy.14
  168.6 0.0 copy-done.5
  168.6 0.8 copy.15
  169.5 10.8 %shard_map.59 = (f32[128,512]{1,0:T(8,128)}, f32[128,512]{1,0:T(8,128)}) custom-call(s32[128,512]{1,0:T(8,128)} %bitcast.32, s32[128,512]{1,0:T(8,128)} %bitcast.33), custom_call_target="tpu_custom_call" | custom-call | tf_op jit(solution)/shard_map/pallas_call | solution.py:212
  180.2 0.0 collective-permute-done.1.other_ref
  180.2 0.0 copy-start.3
  180.2 0.0 copy-done.1
  180.2 0.7 copy-done.3
  181.0 24.5 %shard_map.60 = (f32[512,128]{1,0:T(8,128)}, f32[128,16,128]{2,1,0:T(8,128)}) custom-call(s32[1]{0:T(128)} %bitcast.core_ref, f32[80,8,128]{2,1,0:T(8,128)} %bitcast.30, f32[80,8,128]{2,1,0:T(8,128)} %copy-done.3, f32[128,512]{1,0:T(8,128)} %get-tuple-element.15.start_ref, f32[512,16,128]{2,1,0:T(8,128)} %bitcast.3.fibers_ref.fibers_hbm), custom_call_target="tpu_custom_call" | custom-call | tf_op jit(solution)/shard_map/pallas_call | solution.py:217
  205.5 20.4 %all_to_all.53.slab_ref = f32[32,4,16,128]{3,2,1,0:T(8,128)} all-to-all(f32[32,4,16,128]{3,2,1,0:T(8,128)} %bitcast.31), channel_id=1, replica_groups=mesh['z'=8,'x'=4,'y'=4,'c'=2] {'y','c','x'}, dimensions={0} | all-to-all | bytes 2097152 | tf_op jit(solution)/shard_map/all_to_all | solution.py:226
  225.9 3.5 %shard_map.61 = (f32[80,8,128]{2,1,0:T(8,128)}, f32[80,8,128]{2,1,0:T(8,128)}) custom-call(s32[1]{0:T(128)} %bitcast.core_ref, f32[32,4,16,128]{3,2,1,0:T(8,128)} %all_to_all.53.slab_ref), custom_call_target="tpu_custom_call" | custom-call | tf_op jit(solution)/shard_map/pallas_call | solution.py:173
  229.3 1.3 collective-permute-start.2
  230.7 1.5 collective-permute-done.2
  232.1 1.0 add.7
  233.1 11.4 %all_to_all.54 = f32[16,5,8,128]{3,2,1,0:T(8,128)S(1)} all-to-all(f32[16,5,8,128]{3,2,1,0:T(8,128)S(1)} %bitcast.28), channel_id=1, replica_groups=mesh['z'=8,'x'=4,'y'=4,'c'=2] {'x','y'}, dimensions={0} | all-to-all | bytes 655360 | tf_op jit(solution)/shard_map/all_to_all | solution.py:201
  244.6 10.8 %all_to_all.55 = f32[8,5,8,128]{3,2,1,0:T(8,128)S(1)} all-to-all(f32[8,5,8,128]{3,2,1,0:T(8,128)S(1)} %broadcast_in_dim.14), channel_id=1, replica_groups=mesh['z'=8,'x'=4,'y'=4,'c'=2] {'z'}, dimensions={0} | all-to-all | bytes 327680 | tf_op jit(solution)/shard_map/all_to_all | solution.py:202
  255.4 11.5 %all_to_all.56 = f32[16,5,8,128]{3,2,1,0:T(8,128)S(1)} all-to-all(f32[16,5,8,128]{3,2,1,0:T(8,128)S(1)} %broadcast_in_dim.15), channel_id=1, replica_groups=mesh['z'=8,'x'=4,'y'=4,'c'=2] {'x','y'}, dimensions={0} | all-to-all | bytes 655360 | tf_op jit(solution)/shard_map/all_to_all | solution.py:203
  266.9 0.0 copy-start
  267.0 4.0 %collective-permute-start.3 = (f32[80,8,128]{2,1,0:T(8,128)S(1)}, f32[80,8,128]{2,1,0:T(8,128)S(1)}, u32[]{:S(2)}, u32[]{:S(2)}) collective-permute-start(f32[80,8,128]{2,1,0:T(8,128)S(1)} %bitcast.25), channel_id=1, source_target_pairs={{0,1},{1,0},{2,3},{3,2},{4,5},{5,4},{6,7},{7,6},{8,9},{9,8},{10,11... | collective-permute-start | bytes 983048 | tf_op jit(solution)/shard_map/ppermute | solution.py:195
  270.9 1.3 collective-permute-done.3.other_ref
  272.2 0.0 copy-start.2
  272.2 0.0 copy-done
  272.2 0.7 copy-done.2
  272.9 22.3 %shard_map.62 = (f32[512,128]{1,0:T(8,128)}, f32[8,4,16,128]{3,2,1,0:T(8,128)}) custom-call(s32[1]{0:T(128)} %bitcast.core_ref, f32[80,8,128]{2,1,0:T(8,128)} %bitcast.26, f32[80,8,128]{2,1,0:T(8,128)} %copy-done.2, f32[128,512]{1,0:T(8,128)} %get-tuple-element.20.start_ref, f32[32,4,16,128]{3,2,1,0:T(8,128)} %all_to_all.53.slab_ref), custom_call_target="tpu_custom_call" | custom-call | tf_op jit(solution)/shard_map/pallas_call | solution.py:228
  295.3 10.2 %all_to_all.57 = f32[8,4,16,128]{3,2,1,0:T(8,128)S(1)} all-to-all(f32[8,4,16,128]{3,2,1,0:T(8,128)} %get-tuple-element.22), channel_id=1, replica_groups=mesh['z'=8,'x'=4,'y'=4,'c'=2] {'y','c'}, dimensions={0} | all-to-all | bytes 524288 | tf_op jit(solution)/shard_map/all_to_all | solution.py:236
  305.5 12.6 %all_to_all.58 = f32[8,4,16,128]{3,2,1,0:T(8,128)S(1)} all-to-all(f32[8,4,16,128]{3,2,1,0:T(8,128)S(1)} %all_to_all.57), channel_id=1, replica_groups=mesh['z'=8,'x'=4,'y'=4,'c'=2] {'z'}, dimensions={0} | all-to-all | bytes 524288 | tf_op jit(solution)/shard_map/all_to_all | solution.py:237
  318.0 0.7 copy_bitcast_fusion
  (8 shorter events, 0.2 us)
Async XLA Ops:
  6.6 105.0 %all-to-all-start = ((f32[32,16,16,128]{3,2,1,0:T(8,128)}), f32[32,16,16,128]{3,2,1,0:T(8,128)}, u32[]{:S(2)}, u32[]{:S(2)}) async-start(f32[32,16,16,128]{3,2,1,0:T(8,128)} %bitcast.22), calls=%async_computation | async-start | bytes 8388608 | tf_op jit(solution)/shard_map/all_to_all | solution.py:211
  18.6 149.2 %copy-start.4 = (s32[512,128]{1,0:T(8,128)S(1)}, s32[512,128]{1,0:T(8,128)}, u32[]{:S(2)}) copy-start(s32[512,128]{1,0:T(8,128)} %param.4) | copy-start | bytes 786436
  111.6 57.0 %copy-start.5 = (s32[512,128]{1,0:T(8,128)S(1)}, s32[512,128]{1,0:T(8,128)}, u32[]{:S(2)}) copy-start(s32[512,128]{1,0:T(8,128)} %param.5) | copy-start | bytes 786436
  120.8 3.7 %collective-permute-start = (f32[80,8,128]{2,1,0:T(8,128)}, f32[80,8,128]{2,1,0:T(8,128)S(1)}, u32[]{:S(2)}, u32[]{:S(2)}) collective-permute-start(f32[80,8,128]{2,1,0:T(8,128)} %get-tuple-element.14), channel_id=1, source_target_pairs={{0,1},{1,0},{2,3},{3,2},{4,5},{5,4},{6,7},{7,6},{8,9},{9,8},{10,11... | collective-permute-start | bytes 983048 | tf_op jit(solution)/shard_map/ppermute | solution.py:195
  163.8 16.4 %copy-start.1 = (f32[16,5,8,128]{3,2,1,0:T(8,128)}, f32[16,5,8,128]{3,2,1,0:T(8,128)S(1)}, u32[]{:S(2)}) copy-start(f32[16,5,8,128]{3,2,1,0:T(8,128)S(1)} %all_to_all.52) | copy-start | bytes 983044
  163.8 16.4 %collective-permute-start.1 = (f32[80,8,128]{2,1,0:T(8,128)S(1)}, f32[80,8,128]{2,1,0:T(8,128)S(1)}, u32[]{:S(2)}, u32[]{:S(2)}) collective-permute-start(f32[80,8,128]{2,1,0:T(8,128)S(1)} %bitcast.29), channel_id=1, source_target_pairs={{0,1},{1,0},{2,3},{3,2},{4,5},{5,4},{6,7},{7,6},{8,9},{9,8},{10,11... | collective-permute-start | bytes 983048 | tf_op jit(solution)/shard_map/ppermute | solution.py:195
  180.2 0.7 copy-start.3
  229.3 2.8 collective-permute-start.2
  266.9 5.3 %copy-start = (f32[16,5,8,128]{3,2,1,0:T(8,128)}, f32[16,5,8,128]{3,2,1,0:T(8,128)S(1)}, u32[]{:S(2)}) copy-start(f32[16,5,8,128]{3,2,1,0:T(8,128)S(1)} %all_to_all.56) | copy-start | bytes 983044
  267.0 5.2 %collective-permute-start.3 = (f32[80,8,128]{2,1,0:T(8,128)S(1)}, f32[80,8,128]{2,1,0:T(8,128)S(1)}, u32[]{:S(2)}, u32[]{:S(2)}) collective-permute-start(f32[80,8,128]{2,1,0:T(8,128)S(1)} %bitcast.25), channel_id=1, source_target_pairs={{0,1},{1,0},{2,3},{3,2},{4,5},{5,4},{6,7},{7,6},{8,9},{9,8},{10,11... | collective-permute-start | bytes 983048 | tf_op jit(solution)/shard_map/ppermute | solution.py:195
  272.2 0.7 copy-start.2

commit v3 on v2

--- a/solution.py
+++ b/solution.py
@@ -100,21 +100,36 @@
     other_ref[...] = swap[1]
 
 
-def first_gram_kernel(core_ref, fibers_ref, mine_ref, other_ref, high, low, swap):
-    flat = fibers_ref.reshape(N * 16, 128)
-    for j in range(16):
-        h, l = split(flat[pl.ds(j, N, stride=16), :])
-        high[:, 128 * j : 128 * j + 128] = h
-        low[:, 128 * j : 128 * j + 128] = l
+def pack_kernel(field_ref, out_ref):
+    for i in range(8):
+        block = jnp.concatenate([field_ref[0, i], field_ref[1, i]], axis=0)
+        out_ref[0, :, 0, i, :] = block.T
+
+
+def first_gram_kernel(core_ref, fibers_hbm, mine_ref, other_ref, high_hbm, low_hbm, fibers, high, low, swap, sems, out_sems):
+    copies = [pltpu.make_async_copy(fibers_hbm.at[:, :, p], fibers.at[p], sems.at[p]) for p in range(4)]
+    for copy in copies:
+        copy.start()
+    first_half = lax.broadcasted_iota(jnp.int32, (32, 8, 128), 2) < 64
+    for p in range(4):
+        copies[p].wait()
+        for pair in range(4):
+            one, two = fibers[p, :, 2 * pair], fibers[p, :, 2 * pair + 1]
+            upper = jnp.where(first_half, one, pltpu.roll(two, 64, 2))
+            lower = jnp.where(first_half, pltpu.roll(one, 64, 2), two)
+            h, l = split(jnp.stack([upper, lower], axis=1).reshape(N, 128))
+            at = slice(512 * p + 128 * pair, 512 * p + 128 * pair + 128)
+            high[:, at] = h
+            low[:, at] = l
+    saves = [
+        pltpu.make_async_copy(high, high_hbm, out_sems.at[0]),
+        pltpu.make_async_copy(low, low_hbm, out_sems.at[1]),
+    ]
+    for save in saves:
+        save.start()
     upper_gram(high, low, mine_ref, other_ref, swap, core_ref[0])
-
-
-def second_gram_kernel(core_ref, slab_ref, mine_ref, other_ref, high, low, swap):
-    for a in range(4):
-        h, l = split(slab_ref[:, a].reshape(N, 128))
-        high[:, 128 * a : 128 * a + 128] = h
-        low[:, 128 * a : 128 * a + 128] = l
-    upper_gram(high, low, mine_ref, other_ref, swap, core_ref[0])
+    for save in saves:
+        save.wait()
 
 
 def leading(core_ref, mine_ref, other_ref, start_ref, whole, gram, parts):
@@ -137,51 +152,74 @@
 
 
 def first_basis_kernel(
-    core_ref, mine_ref, other_ref, start_ref, fibers_hbm, basis_ref, reduced_ref, whole, gram, parts, fibers, sem
+    core_ref, mine_ref, other_ref, start_ref, high_hbm, low_hbm,
+    basis_ref, reduced_ref, mine_out, other_out,
+    whole, gram, parts, held, high, low, turned_high, turned_low, sems,
 ):
-    copy = pltpu.make_async_copy(fibers_hbm, fibers, sem)
+    copies = [pltpu.make_async_copy(high_hbm, high, sems.at[0]), pltpu.make_async_copy(low_hbm, low, sems.at[1])]
+    for copy in copies:
+        copy.start()
+    basis = leading(core_ref, mine_ref, other_ref, start_ref, whole, gram, parts)
+    basis_ref[...] = basis.T
+    columns = []
+    for k in range(4):
+        held[k] = basis[:, 128 * k : 128 * k + 128]
+        columns.append(jnp.concatenate([held[k, pl.ds(r, 32, stride=4), :] for r in range(4)], axis=0))
+    basis = jnp.concatenate(columns, axis=1)
+    basis_high, basis_low = split(basis)
+    both = jnp.concatenate([basis_high, basis_low], axis=0)
+    for copy in copies:
+        copy.wait()
+    for p in range(4):
+        at = slice(512 * p, 512 * p + 512)
+        twice = dot(both, high[:, at], NN)
+        reduced = twice[:RANK] + twice[RANK:] + dot(basis_high, low[:, at], NN)
+        reduced_ref[:, at] = reduced
+        h, l = split(reduced.T)
+        turned_high[:, 128 * p : 128 * p + 128] = h
+        turned_low[:, 128 * p : 128 * p + 128] = l
+    upper_gram(turned_high, turned_low, mine_out, other_out, whole, core_ref[0])
+
+
+def second_basis_kernel(
+    core_ref, mine_ref, other_ref, start_ref, reduced_hbm, basis_ref, core_out, whole, gram, parts, reduced, product, sem
+):
+    copy = pltpu.make_async_copy(reduced_hbm, reduced, sem)
     copy.start()
     basis = leading(core_ref, mine_ref, other_ref, start_ref, whole, gram, parts)
     basis_ref[...] = basis.T
-    basis = as_left(basis)
+    basis = as_right_cols(basis)
     copy.wait()
-    flat = fibers.reshape(N * 16, 128)
-    out = reduced_ref.reshape(RANK * 16, 128)
-    for j in range(0, 16, 2):
-        pair = jnp.concatenate([flat[pl.ds(j, N, stride=16), :], flat[pl.ds(j + 1, N, stride=16), :]], axis=1)
-        reduced = dot(basis, as_right_rows(pair), NN)
-        out[pl.ds(j, RANK, stride=16), :] = reduced[:, :128]
-        out[pl.ds(j + 1, RANK, stride=16), :] = reduced[:, 128:]
-
-
-def second_basis_kernel(core_ref, mine_ref, other_ref, start_ref, slab_ref, basis_ref, core_out, whole, gram, parts):
-    basis = leading(core_ref, mine_ref, other_ref, start_ref, whole, gram, parts)
-    basis_ref[...] = basis.T
-    basis = as_left(basis)
-    for a in range(0, 4, 2):
-        pair = jnp.concatenate([slab_ref[:, a].reshape(N, 128), slab_ref[:, a + 1].reshape(N, 128)], axis=1)
-        got = dot(basis, as_right_rows(pair), NN)
-        core_out[:, a] = got[:, :128].reshape(8, 16, 128)
-        core_out[:, a + 1] = got[:, 128:].reshape(8, 16, 128)
+    for p in range(4):
+        product[128 * p : 128 * p + 128, :] = dot(as_left(reduced[:, 512 * p : 512 * p + 512]), basis, NT)
+    row = lax.broadcasted_iota(jnp.int32, (8, 128), 0)
+    group = lax.broadcasted_iota(jnp.int32, (8, 128), 1) // 16
+    for q in range(32):
+        for half in range(2):
+            block = product[pl.ds(q + 256 * half, 8, stride=32), :]
+            for bit in (1, 2, 4):
+                up = pltpu.roll(pltpu.roll(block, 8 - bit, 0), 16 * bit, 1)
+                down = pltpu.roll(pltpu.roll(block, bit, 0), 128 - 16 * bit, 1)
+                same = (row & bit) == (group & bit)
+                block = jnp.where(same, block, jnp.where((row & bit) == 0, up, down))
+            core_out[pl.ds(16 * q + half, 8, stride=2), :] = block
+
+
+def unpack_kernel(got_ref, out_ref):
+    for half in range(2):
+        for part in range(2):
+            block = got_ref[pl.ds(256 * part + half, 128, stride=2), :].T
+            for low in range(2):
+                at = 256 * (2 * half + low) + 128 * part
+                out_ref[:, :, at : at + 128] = block[64 * low : 64 * low + 64].reshape(4, 16, 128)
 
 
 def shaped(*shape):
     return jax.ShapeDtypeStruct(shape, F32)
 
 
-def gram_call(kernel, depth, core, x):
-    return pl.pallas_call(
-        kernel,
-        out_shape=(shaped(HALF, 8, 128), shaped(HALF, 8, 128)),
-        in_specs=[SMEM, VMEM],
-        out_specs=(VMEM, VMEM),
-        scratch_shapes=[
-            pltpu.VMEM((N, depth), BF16),
-            pltpu.VMEM((N, depth), BF16),
-            pltpu.VMEM((2, HALF, 8, 128), F32),
-        ],
-        compiler_params=PARAMS,
-    )(core, x)
+def shaped_half(*shape):
+    return jax.ShapeDtypeStruct(shape, BF16)
 
 
 LEADING_SCRATCH = [
@@ -207,35 +245,67 @@
 
 def local(field, seeds_first, seeds_second):
     core = lax.axis_index("c").reshape(1)
-    sent = field.reshape(16, 4, 16, 8, 128).transpose(3, 1, 0, 2, 4).reshape(32, 16, 16, 128)
-    fibers = lax.all_to_all(sent, ("z", "x"), 0, 0, tiled=True).reshape(N, 16, 128)
+    sent = pl.pallas_call(
+        pack_kernel,
+        grid=(4, 2),
+        out_shape=shaped(2, 128, 4, 8, 128),
+        in_specs=[pl.BlockSpec((2, 8, 64, 128), lambda p, h: (0, 0, 0, 2 * p + h))],
+        out_specs=pl.BlockSpec((1, 128, 1, 8, 128), lambda p, h: (h, 0, p, 0, 0)),
+        compiler_params=PARAMS,
+    )(field.reshape(2, 8, 64, 1024))
+    fibers = lax.all_to_all(sent.reshape(256, 4, 8, 128), ("z", "x", "y", "c"), 0, 0, tiled=True)
     starts = pl.pallas_call(
         seeds_kernel, out_shape=(shaped(RANK, N), shaped(RANK, N)), compiler_params=PARAMS
     )(seeds_first.T, seeds_second.T)
-
-    mine, other = total(*gram_call(first_gram_kernel, 2048, core, fibers))
-    basis_first, reduced = pl.pallas_call(
+    fibers, starts = lax.optimization_barrier((fibers, starts))
+
+    halves = (shaped(HALF, 8, 128), shaped(HALF, 8, 128))
+    mine, other, high, low = pl.pallas_call(
+        first_gram_kernel,
+        out_shape=halves + (shaped_half(N, 2048), shaped_half(N, 2048)),
+        in_specs=[SMEM, ANY],
+        out_specs=(VMEM, VMEM, ANY, ANY),
+        scratch_shapes=[
+            pltpu.VMEM((4, 32, 8, 8, 128), F32),
+            pltpu.VMEM((N, 2048), BF16),
+            pltpu.VMEM((N, 2048), BF16),
+            pltpu.VMEM((2, HALF, 8, 128), F32),
+            pltpu.SemaphoreType.DMA((4,)),
+            pltpu.SemaphoreType.DMA((2,)),
+        ],
+        compiler_params=PARAMS,
+    )(core, fibers.reshape(32, 8, 4, 8, 128))
+    mine, other = total(mine, other)
+    basis_first, reduced, mine, other = pl.pallas_call(
         first_basis_kernel,
-        out_shape=(shaped(N, RANK), shaped(RANK, 16, 128)),
+        out_shape=(shaped(N, RANK), shaped(RANK, 2048)) + halves,
+        in_specs=[SMEM, VMEM, VMEM, VMEM, ANY, ANY],
+        out_specs=(VMEM, VMEM, VMEM, VMEM),
+        scratch_shapes=LEADING_SCRATCH
+        + [
+            pltpu.VMEM((4, RANK, 128), F32),
+            pltpu.VMEM((N, 2048), BF16),
+            pltpu.VMEM((N, 2048), BF16),
+            pltpu.VMEM((N, 4 * RANK), BF16),
+            pltpu.VMEM((N, 4 * RANK), BF16),
+            pltpu.SemaphoreType.DMA((2,)),
+        ],
+        compiler_params=PARAMS,
+    )(core, mine, other, starts[0], high, low)
+    mine, other = total(mine, other)
+    basis_second, ranks = pl.pallas_call(
+        second_basis_kernel,
+        out_shape=(shaped(N, RANK), shaped(512, 128)),
         in_specs=[SMEM, VMEM, VMEM, VMEM, ANY],
         out_specs=(VMEM, VMEM),
-        scratch_shapes=LEADING_SCRATCH + [pltpu.VMEM((N, 16, 128), F32), pltpu.SemaphoreType.DMA],
+        scratch_shapes=LEADING_SCRATCH
+        + [pltpu.VMEM((RANK, 2048), F32), pltpu.VMEM((4 * RANK, RANK), F32), pltpu.SemaphoreType.DMA],
         compiler_params=PARAMS,
-    )(core, mine, other, starts[0], fibers)
-
-    slab = lax.all_to_all(reduced.reshape(32, 4, 16, 128), ("y", "c", "x"), 0, 0, tiled=True)
-    mine, other = total(*gram_call(second_gram_kernel, 512, core, slab))
-    basis_second, ranks = pl.pallas_call(
-        second_basis_kernel,
-        out_shape=(shaped(N, RANK), shaped(8, 4, 16, 128)),
-        in_specs=[SMEM, VMEM, VMEM, VMEM, VMEM],
-        out_specs=(VMEM, VMEM),
-        scratch_shapes=LEADING_SCRATCH,
-        compiler_params=PARAMS,
-    )(core, mine, other, starts[1], slab)
-    ranks = lax.all_to_all(ranks, ("y", "c"), 0, 0, tiled=True)
-    ranks = lax.all_to_all(ranks, "z", 0, 0, tiled=True)
-    core_tensor = ranks.transpose(1, 2, 0, 3).reshape(4, 16, 1024)
+    )(core, mine, other, starts[1], reduced)
+    ranks = lax.all_to_all(ranks.reshape(256, 2, 128), ("z", "x", "y", "c"), 0, 0, tiled=True)
+    core_tensor = pl.pallas_call(unpack_kernel, out_shape=shaped(4, 16, 1024), compiler_params=PARAMS)(
+        ranks.reshape(512, 128)
+    )
     return (basis_first, basis_second, core_tensor)
 
 

time: 320 us -> 287 us (0.90)
  blocking collectives: 115 us -> 89.6 us
  waiting for transfers between devices: 97.2 us -> 89.5 us
  local copies, waits for them, and re-layouts: 9.87 us -> 3.22 us
  Pallas kernels: 70.3 us -> 75.1 us
    all_to_all x3 -> x1, blocking collectives: 43.1 us -> 21.9 us  [local(): lax.all_to_all(ranks.reshape(256, 2, 128), ('z', 'x', 'y', 'c'), 0, 0, ti...]
    all_to_all x1, waiting for transfers between devices: 93 us -> 84.1 us  [local(): lax.all_to_all(sent.reshape(256, 4, 8, 128), ('z', 'x', 'y', 'c'), 0, 0,...]
    pallas_call x3 -> x4, Pallas kernels: 35 us -> 40.4 us  [the longest x1 22.4 us: local(): pl.pallas_call(second_basis_kernel, out_shape=(shaped(N, RANK), shaped(51...]
    all_to_all x1, starting transfers between devices: 12 us -> 16.7 us  [local(): lax.all_to_all(sent.reshape(256, 4, 8, 128), ('z', 'x', 'y', 'c'), 0, 0,...]
    all_to_all x2, blocking collectives: 27.2 us -> 23 us  [total(): got = jnp.sum(lax.all_to_all(mine, ('x', 'y'), 0, 0, tiled=True), axis=0)]
  transfers between devices with their start and end apart: 5 -> 5, of which waited for: 4 -> 5; matrix products, arithmetic and copies ran while one was open for 1% -> 1% of each run, Pallas kernels for 3% -> 4%
where the time goes in v3:
time: 287 us
  blocking collectives  89.6 us (31%)
  waiting for transfers between devices  89.5 us (31%)
  Pallas kernels  75.1 us (26%)
  starting transfers between devices  26.5 us (9%)
  local copies, waits for them, and re-layouts  3.22 us (1%)
    all_to_all x1, waiting for transfers between devices, local(): lax.all_to_all(sent.reshape(256, 4, 8, 128), ('z', 'x', 'y', 'c'), 0, 0,...  84.1 us
    pallas_call x1, Pallas kernels, local(): pl.pallas_call(first_basis_kernel, out_shape=(shaped(N, RANK), shaped(RAN...  23.9 us
    all_to_all x2, blocking collectives, total(): lax.all_to_all(jnp.broadcast_to(got, (16, share, 8, 128)), ('x', 'y'), 0,...  23.2 us
    all_to_all x2, blocking collectives, total(): got = jnp.sum(lax.all_to_all(mine, ('x', 'y'), 0, 0, tiled=True), axis=0)  23 us
    pallas_call x1, Pallas kernels, local(): pl.pallas_call(second_basis_kernel, out_shape=(shaped(N, RANK), shaped(51...  22.4 us
    all_to_all x1, blocking collectives, local(): lax.all_to_all(ranks.reshape(256, 2, 128), ('z', 'x', 'y', 'c'), 0, 0, ti...  21.9 us
    all_to_all x2, blocking collectives, total(): lax.all_to_all(jnp.broadcast_to(got, (8, share, 8, 128)), 'z', 0, 0, tile...  21.5 us
    all_to_all x1, starting transfers between devices, local(): lax.all_to_all(sent.reshape(256, 4, 8, 128), ('z', 'x', 'y', 'c'), 0, 0,...  16.7 us
  transfers between devices with their start and end apart: 5, of which 5 were waited for; matrix products, arithmetic and copies ran while one was open for 1% of the time, Pallas kernels for 4%

profile of v3, /device:TPU:1, one launch (start us, length us, event | category | flops | bytes accessed | tf_op | source)
XLA Modules:
  0.0 286.7 jit_solution(10934755368176499192)
XLA Ops:
  0.6 7.8 %shard_map.58 = f32[2,128,4,8,128]{4,3,2,1,0:T(8,128)} custom-call(f32[2,8,64,1024]{3,2,1,0:T(8,128)} %bitcast.13), custom_call_target="tpu_custom_call" | custom-call | tf_op jit(solution)/shard_map/pallas_call | solution.py:248
  8.4 0.0 copy-start.4
  8.4 0.0 copy-start.5
  8.4 16.7 %all-to-all-start = ((f32[256,4,8,128]{3,2,1,0:T(8,128)}), f32[256,4,8,128]{3,2,1,0:T(8,128)}, u32[]{:S(2)}, u32[]{:S(2)}) async-start(f32[256,4,8,128]{3,2,1,0:T(8,128)} %bitcast.12), calls=%async_computation | async-start | bytes 8388608 | tf_op jit(solution)/shard_map/all_to_all | solution.py:256
  25.1 0.0 copy-done.4
  25.1 0.8 copy.8
  25.9 0.0 copy-done.5
  25.9 0.8 copy.9
  26.8 10.8 %shard_map.59 = (f32[128,512]{1,0:T(8,128)}, f32[128,512]{1,0:T(8,128)}) custom-call(s32[128,512]{1,0:T(8,128)} %bitcast.20, s32[128,512]{1,0:T(8,128)} %bitcast.21), custom_call_target="tpu_custom_call" | custom-call | tf_op jit(solution)/shard_map/pallas_call | solution.py:257
  37.5 84.1 %all-to-all-done = f32[256,4,8,128]{3,2,1,0:T(8,128)} async-done(((f32[256,4,8,128]{3,2,1,0:T(8,128)}), f32[256,4,8,128]{3,2,1,0:T(8,128)}, u32[]{:S(2)}, u32[]{:S(2)}) %all-to-all-start) | async-done | bytes 4194336 | tf_op jit(solution)/shard_map/all_to_all | solution.py:256
  121.6 8.4 %shard_map.60 = (f32[80,8,128]{2,1,0:T(8,128)}, f32[80,8,128]{2,1,0:T(8,128)}, bf16[512,2048]{1,0:T(8,128)(2,1)}, bf16[512,2048]{1,0:T(8,128)(2,1)}) custom-call(s32[1]{0:T(128)} %bitcast.core_ref, f32[32,8,4,8,128]{4,3,2,1,0:T(8,128)} %bitcast.5.fibers_hbm), custom_call_target="tpu_custom_call" | custom-call | tf_op jit(solution)/shard_map/pallas_call | solution.py:263
  130.0 1.3 collective-permute-start
  131.3 1.5 collective-permute-done
  132.8 1.0 add.6
  133.8 11.9 %all_to_all.40 = f32[16,5,8,128]{3,2,1,0:T(8,128)S(1)} all-to-all(f32[16,5,8,128]{3,2,1,0:T(8,128)S(1)} %bitcast.16), channel_id=1, replica_groups=mesh['z'=8,'x'=4,'y'=4,'c'=2] {'x','y'}, dimensions={0} | all-to-all | bytes 655360 | tf_op jit(solution)/shard_map/all_to_all | solution.py:239
  145.8 10.8 %all_to_all.41 = f32[8,5,8,128]{3,2,1,0:T(8,128)S(1)} all-to-all(f32[8,5,8,128]{3,2,1,0:T(8,128)S(1)} %broadcast_in_dim.12), channel_id=1, replica_groups=mesh['z'=8,'x'=4,'y'=4,'c'=2] {'z'}, dimensions={0} | all-to-all | bytes 327680 | tf_op jit(solution)/shard_map/all_to_all | solution.py:240
  156.6 11.6 %all_to_all.42 = f32[16,5,8,128]{3,2,1,0:T(8,128)S(1)} all-to-all(f32[16,5,8,128]{3,2,1,0:T(8,128)S(1)} %broadcast_in_dim.13), channel_id=1, replica_groups=mesh['z'=8,'x'=4,'y'=4,'c'=2] {'x','y'}, dimensions={0} | all-to-all | bytes 655360 | tf_op jit(solution)/shard_map/all_to_all | solution.py:241
  168.2 0.0 copy-start.1
  168.2 4.0 %collective-permute-start.1 = (f32[80,8,128]{2,1,0:T(8,128)S(1)}, f32[80,8,128]{2,1,0:T(8,128)S(1)}, u32[]{:S(2)}, u32[]{:S(2)}) collective-permute-start(f32[80,8,128]{2,1,0:T(8,128)S(1)} %bitcast.18), channel_id=1, source_target_pairs={{0,1},{1,0},{2,3},{3,2},{4,5},{5,4},{6,7},{7,6},{8,9},{9,8},{10,11... | collective-permute-start | bytes 983048 | tf_op jit(solution)/shard_map/ppermute | solution.py:233
  172.2 1.3 collective-permute-done.1.other_ref
  173.5 0.0 copy-start.3
  173.5 0.0 copy-done.1
  173.5 0.7 copy-done.3
  174.2 23.9 %shard_map.61 = (f32[512,128]{1,0:T(8,128)}, f32[128,2048]{1,0:T(8,128)}, f32[80,8,128]{2,1,0:T(8,128)}, f32[80,8,128]{2,1,0:T(8,128)}) custom-call(s32[1]{0:T(128)} %bitcast.core_ref, f32[80,8,128]{2,1,0:T(8,128)} %bitcast.19, f32[80,8,128]{2,1,0:T(8,128)} %copy-done.3, f32[128,512]{1,0:T(8,128)} %get-tuple-element.23.start_ref, ...), custom_call_target="tpu_custom_call" | custom-call | tf_op jit(solution)/shard_map/pallas_call | solution.py:279
  198.2 0.5 collective-permute-start.2
  198.6 1.5 collective-permute-done.2
  200.1 1.0 add.7
  201.1 11.1 %all_to_all.43 = f32[16,5,8,128]{3,2,1,0:T(8,128)S(1)} all-to-all(f32[16,5,8,128]{3,2,1,0:T(8,128)S(1)} %bitcast.17), channel_id=1, replica_groups=mesh['z'=8,'x'=4,'y'=4,'c'=2] {'x','y'}, dimensions={0} | all-to-all | bytes 655360 | tf_op jit(solution)/shard_map/all_to_all | solution.py:239
  212.3 10.8 %all_to_all.44 = f32[8,5,8,128]{3,2,1,0:T(8,128)S(1)} all-to-all(f32[8,5,8,128]{3,2,1,0:T(8,128)S(1)} %broadcast_in_dim.14), channel_id=1, replica_groups=mesh['z'=8,'x'=4,'y'=4,'c'=2] {'z'}, dimensions={0} | all-to-all | bytes 327680 | tf_op jit(solution)/shard_map/all_to_all | solution.py:240
  223.1 11.5 %all_to_all.45 = f32[16,5,8,128]{3,2,1,0:T(8,128)S(1)} all-to-all(f32[16,5,8,128]{3,2,1,0:T(8,128)S(1)} %broadcast_in_dim.15), channel_id=1, replica_groups=mesh['z'=8,'x'=4,'y'=4,'c'=2] {'x','y'}, dimensions={0} | all-to-all | bytes 655360 | tf_op jit(solution)/shard_map/all_to_all | solution.py:241
  234.7 0.0 copy-start
  234.7 4.0 %collective-permute-start.3 = (f32[80,8,128]{2,1,0:T(8,128)S(1)}, f32[80,8,128]{2,1,0:T(8,128)S(1)}, u32[]{:S(2)}, u32[]{:S(2)}) collective-permute-start(f32[80,8,128]{2,1,0:T(8,128)S(1)} %bitcast.14), channel_id=1, source_target_pairs={{0,1},{1,0},{2,3},{3,2},{4,5},{5,4},{6,7},{7,6},{8,9},{9,8},{10,11... | collective-permute-start | bytes 983048 | tf_op jit(solution)/shard_map/ppermute | solution.py:233
  238.6 1.3 collective-permute-done.3.other_ref
  239.9 0.0 copy-start.2
  239.9 0.0 copy-done
  239.9 0.7 copy-done.2
  240.6 22.4 %shard_map.62 = (f32[512,128]{1,0:T(8,128)}, f32[512,128]{1,0:T(8,128)}) custom-call(s32[1]{0:T(128)} %bitcast.core_ref, f32[80,8,128]{2,1,0:T(8,128)} %bitcast.15, f32[80,8,128]{2,1,0:T(8,128)} %copy-done.2, f32[128,512]{1,0:T(8,128)} %get-tuple-element.29.start_ref, f32[128,2048]{1,0:T(8,128)} %get-tuple-element.30.reduced_hbm), custom_call_target="tpu_custom_call" | custom-call | tf_op jit(solution)/shard_map/pallas_call | solution.py:296
  263.0 21.9 %all_to_all.46 = f32[256,2,128]{2,1,0:T(2,128)} all-to-all(f32[256,2,128]{2,1,0:T(2,128)} %bitcast.23), channel_id=1, replica_groups=mesh['z'=8,'x'=4,'y'=4,'c'=2] {'z','x','y','c'}, dimensions={0} | all-to-all | bytes 524288 | tf_op jit(solution)/shard_map/all_to_all | solution.py:305
  284.9 1.8 shard_map.63
  (8 shorter events, 0.2 us)
Async XLA Ops:
  8.4 16.7 %copy-start.4 = (s32[512,128]{1,0:T(8,128)S(1)}, s32[512,128]{1,0:T(8,128)}, u32[]{:S(2)}) copy-start(s32[512,128]{1,0:T(8,128)} %param.4) | copy-start | bytes 786436
  8.4 17.5 %copy-start.5 = (s32[512,128]{1,0:T(8,128)S(1)}, s32[512,128]{1,0:T(8,128)}, u32[]{:S(2)}) copy-start(s32[512,128]{1,0:T(8,128)} %param.5) | copy-start | bytes 786436
  8.4 113.2 %all-to-all-start = ((f32[256,4,8,128]{3,2,1,0:T(8,128)}), f32[256,4,8,128]{3,2,1,0:T(8,128)}, u32[]{:S(2)}, u32[]{:S(2)}) async-start(f32[256,4,8,128]{3,2,1,0:T(8,128)} %bitcast.12), calls=%async_computation | async-start | bytes 8388608 | tf_op jit(solution)/shard_map/all_to_all | solution.py:256
  130.0 2.8 collective-permute-start
  168.2 5.3 %copy-start.1 = (f32[16,5,8,128]{3,2,1,0:T(8,128)}, f32[16,5,8,128]{3,2,1,0:T(8,128)S(1)}, u32[]{:S(2)}) copy-start(f32[16,5,8,128]{3,2,1,0:T(8,128)S(1)} %all_to_all.42) | copy-start | bytes 983044
  168.2 5.3 %collective-permute-start.1 = (f32[80,8,128]{2,1,0:T(8,128)S(1)}, f32[80,8,128]{2,1,0:T(8,128)S(1)}, u32[]{:S(2)}, u32[]{:S(2)}) collective-permute-start(f32[80,8,128]{2,1,0:T(8,128)S(1)} %bitcast.18), channel_id=1, source_target_pairs={{0,1},{1,0},{2,3},{3,2},{4,5},{5,4},{6,7},{7,6},{8,9},{9,8},{10,11... | collective-permute-start | bytes 983048 | tf_op jit(solution)/shard_map/ppermute | solution.py:233
  173.5 0.7 copy-start.3
  198.2 1.9 collective-permute-start.2
  234.7 5.2 %copy-start = (f32[16,5,8,128]{3,2,1,0:T(8,128)}, f32[16,5,8,128]{3,2,1,0:T(8,128)S(1)}, u32[]{:S(2)}) copy-start(f32[16,5,8,128]{3,2,1,0:T(8,128)S(1)} %all_to_all.45) | copy-start | bytes 983044
  234.7 5.2 %collective-permute-start.3 = (f32[80,8,128]{2,1,0:T(8,128)S(1)}, f32[80,8,128]{2,1,0:T(8,128)S(1)}, u32[]{:S(2)}, u32[]{:S(2)}) collective-permute-start(f32[80,8,128]{2,1,0:T(8,128)S(1)} %bitcast.14), channel_id=1, source_target_pairs={{0,1},{1,0},{2,3},{3,2},{4,5},{5,4},{6,7},{7,6},{8,9},{9,8},{10,11... | collective-permute-start | bytes 983048 | tf_op jit(solution)/shard_map/ppermute | solution.py:233
  239.9 0.7 copy-start.2

commit v4 on v3

--- a/solution.py
+++ b/solution.py
@@ -44,83 +44,119 @@
     return jnp.concatenate([high, high, low], axis=1)
 
 
-def inverse_factor(inner):
+def inverse_factor(inner, one):
     sub = lax.broadcasted_iota(jnp.int32, (8, RANK), 0)
     lane = lax.broadcasted_iota(jnp.int32, (8, RANK), 1)
-    panels = RANK // 8
-    left = [inner[8 * i : 8 * i + 8, :] for i in range(panels)]
-    right = [jnp.where(lane == sub + 8 * i, 1.0, 0.0).astype(F32) for i in range(panels)]
     spread = lambda row: jnp.broadcast_to(row, (8, RANK))
+    rest = [inner[8 * i : 8 * i + 8, :] for i in range(RANK // 8)]
     out = []
-    for p in range(panels):
-        rows = range(p, panels)
-        cols = {i: [spread(left[i][:, 8 * p + t : 8 * p + t + 1]) for t in range(8)] for i in rows}
-        done = jnp.zeros((8, RANK), F32)
-        for t in range(8):
-            root = lax.rsqrt(spread(cols[p][t][t : t + 1, :]))
-            left_row = spread(left[p][t : t + 1, :]) * root
-            right_row = spread(right[p][t : t + 1, :]) * root
-            done = jnp.where(sub == t, right_row, done)
-            ahead = [spread(cols[p][u][t : t + 1, :]) * root for u in range(t + 1, 8)]
+    for last in (8, 16):
+        factor = []
+        for p in range(last - 8, last):
+            rows = range(p, last)
+            cols = {i: [spread(rest[i][:, 8 * p + t : 8 * p + t + 1]) for t in range(8)] for i in rows}
+            cols[p] = [col * one for col in cols[p]]
+            panel = (lane >= 8 * p) & (lane < 8 * p + 8)
             for i in rows:
-                factor = cols[i][t] * root
-                left[i] = left[i] - factor * left_row
-                right[i] = right[i] - factor * right_row
-                for k, u in enumerate(range(t + 1, 8)):
-                    cols[i][u] = cols[i][u] - factor * ahead[k]
-        out.append(done)
+                unit = jnp.where(lane == sub + 8 * p, 1.0, 0.0) if i == p else 0.0
+                rest[i] = jnp.where(panel, unit, rest[i])
+            done = jnp.zeros((8, RANK), F32)
+            pivots = jnp.ones((8, RANK), F32)
+            for t in range(8):
+                pivot = spread(cols[p][t][t : t + 1, :])
+                row = spread(rest[p][t : t + 1, :])
+                done = jnp.where(sub == t, row, done)
+                pivots = jnp.where(sub == t, pivot, pivots)
+                inverse = 1.0 / pivot
+                ahead = [spread(cols[p][u][t : t + 1, :]) for u in range(t + 1, 8)]
+                for i in rows:
+                    scaled = cols[i][t] * inverse
+                    for k, u in enumerate(range(t + 1, 8)):
+                        cols[i][u] = cols[i][u] - scaled * ahead[k]
+                    if i > p or t < 7:
+                        rest[i] = rest[i] - scaled * row
+            done = done * lax.rsqrt(pivots)
+            out.append(jnp.where(lane < 8 * p + 8, done, 0.0))
+            factor.append(jnp.where((lane < 8 * p + 8) | (lane >= 8 * last), done, 0.0))
+        if last < 16:
+            factor = jnp.concatenate(factor, axis=0)
+            change = lax.dot_general(
+                factor[:, 8 * last :],
+                factor,
+                (((0,), (0,)), ((), ())),
+                precision=lax.Precision.HIGHEST,
+                preferred_element_type=F32,
+            )
+            for k, i in enumerate(range(last, 16)):
+                rest[i] = jnp.where(lane < 8 * last, 0.0, rest[i]) - change[8 * k : 8 * k + 8]
     return jnp.concatenate(out, axis=0)
 
 
-def orthonormal(turned):
+def ones(core_ref):
+    return jnp.full((8, RANK), jnp.minimum(core_ref[0] + 1, 1).astype(F32))
+
+
+def orthonormal(turned, one):
     inner = dot(as_left(turned), as_right_cols(turned), NT)
-    return dot(as_left(inverse_factor(inner)), as_right_rows(turned), NN)
-
-
-def seeds_kernel(first_ref, second_ref, first_out, second_out):
-    first_out[...] = orthonormal(first_ref[...].astype(F32))
-    second_out[...] = orthonormal(second_ref[...].astype(F32))
+    return dot(as_left(inverse_factor(inner, one)), as_right_rows(turned), NN)
+
+
+def seeds_kernel(core_ref, first_ref, second_ref, first_out, second_out):
+    one = ones(core_ref)
+    first_out[...] = orthonormal(first_ref[...].astype(F32), one)
+    second_out[...] = orthonormal(second_ref[...].astype(F32), one)
 
 
 def upper_gram(high, low, mine_ref, other_ref, swap, core):
-    for block in range(4):
-        rows = slice(128 * block, 128 * block + 128)
-        cols = slice(128 * block, N)
-        gram = dot(
-            jnp.concatenate([high[rows, :], low[rows, :], high[rows, :]], axis=1),
-            jnp.concatenate([high[cols, :], high[cols, :], low[cols, :]], axis=1),
-            NT,
-        )
+    for block in range(2):
+        rows, cols = slice(0, 256 * block + 256), slice(256 * block, 256 * block + 256)
+        gram = dot(high[rows, :], high[cols, :], NT)
+        gram += dot(low[rows, :], high[cols, :], NT)
+        gram += dot(high[rows, :], low[cols, :], NT)
         for at, (row, col) in enumerate(TILES):
-            if row // 16 == block:
-                r, c = 8 * (row % 16), 128 * (col - block)
+            if col // 2 == block:
+                r, c = 8 * row, 128 * (col % 2)
                 half = lax.bitwise_xor(at // HALF, core)
                 swap[half, at % HALF] = gram[r : r + 8, c : c + 128]
     mine_ref[...] = swap[0]
     other_ref[...] = swap[1]
 
 
-def pack_kernel(field_ref, out_ref):
-    for i in range(8):
-        block = jnp.concatenate([field_ref[0, i], field_ref[1, i]], axis=0)
-        out_ref[0, :, 0, i, :] = block.T
+def pack_kernel(field_hbm, out_hbm, field, out, sems, out_sems):
+    copies = [pltpu.make_async_copy(field_hbm.at[:, i], field.at[:, i], sems.at[i]) for i in range(8)]
+    for copy in copies:
+        copy.start()
+    saves = []
+    for half in range(2):
+        for i in range(8):
+            if half == 0:
+                copies[i].wait()
+            for p in range(4):
+                at = slice(256 * p + 128 * half, 256 * p + 128 * half + 128)
+                out[half, :, p, i, :] = jnp.concatenate([field[0, i, :, at], field[1, i, :, at]], axis=0).T
+        saves.append(pltpu.make_async_copy(out.at[half], out_hbm.at[half], out_sems.at[half]))
+        saves[half].start()
+    for save in saves:
+        save.wait()
 
 
 def first_gram_kernel(core_ref, fibers_hbm, mine_ref, other_ref, high_hbm, low_hbm, fibers, high, low, swap, sems, out_sems):
-    copies = [pltpu.make_async_copy(fibers_hbm.at[:, :, p], fibers.at[p], sems.at[p]) for p in range(4)]
+    quarters = [slice(8 * q, 8 * q + 8) for q in range(4)]
+    copies = [pltpu.make_async_copy(fibers_hbm.at[at], fibers.at[at], sems.at[q]) for q, at in enumerate(quarters)]
     for copy in copies:
         copy.start()
-    first_half = lax.broadcasted_iota(jnp.int32, (32, 8, 128), 2) < 64
-    for p in range(4):
-        copies[p].wait()
-        for pair in range(4):
-            one, two = fibers[p, :, 2 * pair], fibers[p, :, 2 * pair + 1]
-            upper = jnp.where(first_half, one, pltpu.roll(two, 64, 2))
-            lower = jnp.where(first_half, pltpu.roll(one, 64, 2), two)
-            h, l = split(jnp.stack([upper, lower], axis=1).reshape(N, 128))
-            at = slice(512 * p + 128 * pair, 512 * p + 128 * pair + 128)
-            high[:, at] = h
-            low[:, at] = l
+    first_half = lax.broadcasted_iota(jnp.int32, (8, 8, 128), 2) < 64
+    for q in range(4):
+        copies[q].wait()
+        for p in range(4):
+            for pair in range(4):
+                one, two = fibers[quarters[q], 2 * pair, p], fibers[quarters[q], 2 * pair + 1, p]
+                upper = jnp.where(first_half, one, pltpu.roll(two, 64, 2))
+                lower = jnp.where(first_half, pltpu.roll(one, 64, 2), two)
+                h, l = split(jnp.stack([upper, lower], axis=1).reshape(128, 128))
+                at = slice(512 * p + 128 * pair, 512 * p + 128 * pair + 128)
+                high[128 * q : 128 * q + 128, at] = h
+                low[128 * q : 128 * q + 128, at] = l
     saves = [
         pltpu.make_async_copy(high, high_hbm, out_sems.at[0]),
         pltpu.make_async_copy(low, low_hbm, out_sems.at[1]),
@@ -132,10 +168,17 @@
         save.wait()
 
 
-def leading(core_ref, mine_ref, other_ref, start_ref, whole, gram, parts):
+def leading(core_ref, mine_hbm, other_hbm, start_ref, whole, gram, parts, tile_sems):
     core = core_ref[0]
-    whole[core] = mine_ref[...]
-    whole[1 - core] = other_ref[...]
+    one = ones(core_ref)
+    copies = [
+        pltpu.make_async_copy(mine_hbm, whole.at[core], tile_sems.at[0]),
+        pltpu.make_async_copy(other_hbm, whole.at[1 - core], tile_sems.at[1]),
+    ]
+    for copy in copies:
+        copy.start()
+    for copy in copies:
+        copy.wait()
     for at, (row, col) in enumerate(TILES):
         gram[8 * row : 8 * row + 8, 128 * col : 128 * col + 128] = whole[at // HALF, at % HALF]
     for row in range(1, 4):
@@ -146,7 +189,7 @@
     parts[...] = as_right_rows(gram[...])
 
     def sweep(_, basis):
-        return orthonormal(dot(as_left(basis), parts[...], NN))
+        return orthonormal(dot(as_left(basis), parts[...], NN), one)
 
     return lax.fori_loop(0, ITERS, sweep, start_ref[...])
 
@@ -154,12 +197,12 @@
 def first_basis_kernel(
     core_ref, mine_ref, other_ref, start_ref, high_hbm, low_hbm,
     basis_ref, reduced_ref, mine_out, other_out,
-    whole, gram, parts, held, high, low, turned_high, turned_low, sems,
+    whole, gram, parts, tile_sems, held, high, low, turned_high, turned_low, sems,
 ):
     copies = [pltpu.make_async_copy(high_hbm, high, sems.at[0]), pltpu.make_async_copy(low_hbm, low, sems.at[1])]
     for copy in copies:
         copy.start()
-    basis = leading(core_ref, mine_ref, other_ref, start_ref, whole, gram, parts)
+    basis = leading(core_ref, mine_ref, other_ref, start_ref, whole, gram, parts, tile_sems)
     basis_ref[...] = basis.T
     columns = []
     for k in range(4):
@@ -182,11 +225,12 @@
 
 
 def second_basis_kernel(
-    core_ref, mine_ref, other_ref, start_ref, reduced_hbm, basis_ref, core_out, whole, gram, parts, reduced, product, sem
+    core_ref, mine_ref, other_ref, start_ref, reduced_hbm, basis_ref, core_out,
+    whole, gram, parts, tile_sems, reduced, product, sem
 ):
     copy = pltpu.make_async_copy(reduced_hbm, reduced, sem)
     copy.start()
-    basis = leading(core_ref, mine_ref, other_ref, start_ref, whole, gram, parts)
+    basis = leading(core_ref, mine_ref, other_ref, start_ref, whole, gram, parts, tile_sems)
     basis_ref[...] = basis.T
     basis = as_right_cols(basis)
     copy.wait()
@@ -226,6 +270,7 @@
     pltpu.VMEM((2, HALF, 8, 128), F32),
     pltpu.VMEM((N, N), F32),
     pltpu.VMEM((3 * N, N), BF16),
+    pltpu.SemaphoreType.DMA((2,)),
 ]
 
 
@@ -247,16 +292,24 @@
     core = lax.axis_index("c").reshape(1)
     sent = pl.pallas_call(
         pack_kernel,
-        grid=(4, 2),
         out_shape=shaped(2, 128, 4, 8, 128),
-        in_specs=[pl.BlockSpec((2, 8, 64, 128), lambda p, h: (0, 0, 0, 2 * p + h))],
-        out_specs=pl.BlockSpec((1, 128, 1, 8, 128), lambda p, h: (h, 0, p, 0, 0)),
+        in_specs=[ANY],
+        out_specs=ANY,
+        scratch_shapes=[
+            pltpu.VMEM((2, 8, 64, 1024), F32),
+            pltpu.VMEM((2, 128, 4, 8, 128), F32),
+            pltpu.SemaphoreType.DMA((8,)),
+            pltpu.SemaphoreType.DMA((2,)),
+        ],
         compiler_params=PARAMS,
     )(field.reshape(2, 8, 64, 1024))
     fibers = lax.all_to_all(sent.reshape(256, 4, 8, 128), ("z", "x", "y", "c"), 0, 0, tiled=True)
     starts = pl.pallas_call(
-        seeds_kernel, out_shape=(shaped(RANK, N), shaped(RANK, N)), compiler_params=PARAMS
-    )(seeds_first.T, seeds_second.T)
+        seeds_kernel,
+        out_shape=(shaped(RANK, N), shaped(RANK, N)),
+        in_specs=[SMEM, VMEM, VMEM],
+        compiler_params=PARAMS,
+    )(core, seeds_first.T, seeds_second.T)
     fibers, starts = lax.optimization_barrier((fibers, starts))
 
     halves = (shaped(HALF, 8, 128), shaped(HALF, 8, 128))
@@ -266,7 +319,7 @@
         in_specs=[SMEM, ANY],
         out_specs=(VMEM, VMEM, ANY, ANY),
         scratch_shapes=[
-            pltpu.VMEM((4, 32, 8, 8, 128), F32),
+            pltpu.VMEM((32, 8, 4, 8, 128), F32),
             pltpu.VMEM((N, 2048), BF16),
             pltpu.VMEM((N, 2048), BF16),
             pltpu.VMEM((2, HALF, 8, 128), F32),
@@ -279,7 +332,7 @@
     basis_first, reduced, mine, other = pl.pallas_call(
         first_basis_kernel,
         out_shape=(shaped(N, RANK), shaped(RANK, 2048)) + halves,
-        in_specs=[SMEM, VMEM, VMEM, VMEM, ANY, ANY],
+        in_specs=[SMEM, ANY, ANY, VMEM, ANY, ANY],
         out_specs=(VMEM, VMEM, VMEM, VMEM),
         scratch_shapes=LEADING_SCRATCH
         + [
@@ -296,7 +349,7 @@
     basis_second, ranks = pl.pallas_call(
         second_basis_kernel,
         out_shape=(shaped(N, RANK), shaped(512, 128)),
-        in_specs=[SMEM, VMEM, VMEM, VMEM, ANY],
+        in_specs=[SMEM, ANY, ANY, VMEM, ANY],
         out_specs=(VMEM, VMEM),
         scratch_shapes=LEADING_SCRATCH
         + [pltpu.VMEM((RANK, 2048), F32), pltpu.VMEM((4 * RANK, RANK), F32), pltpu.SemaphoreType.DMA],

time: 287 us -> 281 us (0.979)
  Pallas kernels: 75.1 us -> 67.4 us
  transfers between devices with their start and end apart: 5 -> 5, of which waited for: 5 -> 5; matrix products, arithmetic and copies ran while one was open for 1% -> 1% of each run, Pallas kernels for 4% -> 3%
where the time goes in v4:
time: 281 us
  waiting for transfers between devices  91 us (32%)
  blocking collectives  89.6 us (32%)
  Pallas kernels  67.4 us (24%)
  starting transfers between devices  26.6 us (9%)
  local copies, waits for them, and re-layouts  3.23 us (1%)
    all_to_all x1, waiting for transfers between devices, local(): lax.all_to_all(sent.reshape(256, 4, 8, 128), ('z', 'x', 'y', 'c'), 0, 0,...  85.6 us
    pallas_call x1, Pallas kernels, local(): pl.pallas_call(first_basis_kernel, out_shape=(shaped(N, RANK), shaped(RAN...  23.4 us
    all_to_all x2, blocking collectives, total(): lax.all_to_all(jnp.broadcast_to(got, (16, share, 8, 128)), ('x', 'y'), 0,...  23.2 us
    all_to_all x2, blocking collectives, total(): got = jnp.sum(lax.all_to_all(mine, ('x', 'y'), 0, 0, tiled=True), axis=0)  23 us
    all_to_all x1, blocking collectives, local(): lax.all_to_all(ranks.reshape(256, 2, 128), ('z', 'x', 'y', 'c'), 0, 0, ti...  21.9 us
    all_to_all x2, blocking collectives, total(): lax.all_to_all(jnp.broadcast_to(got, (8, share, 8, 128)), 'z', 0, 0, tile...  21.5 us
    pallas_call x1, Pallas kernels, local(): pl.pallas_call(second_basis_kernel, out_shape=(shaped(N, RANK), shaped(51...  21.1 us
    all_to_all x1, starting transfers between devices, local(): lax.all_to_all(sent.reshape(256, 4, 8, 128), ('z', 'x', 'y', 'c'), 0, 0,...  16.7 us
  transfers between devices with their start and end apart: 5, of which 5 were waited for; matrix products, arithmetic and copies ran while one was open for 1% of the time, Pallas kernels for 3%

profile of v4, /device:TPU:1, one launch (start us, length us, event | category | flops | bytes accessed | tf_op | source)
XLA Modules:
  0.0 280.8 jit_solution(12686028227342318164)
XLA Ops:
  0.6 5.7 %shard_map.58 = f32[2,128,4,8,128]{4,3,2,1,0:T(8,128)} custom-call(f32[2,8,64,1024]{3,2,1,0:T(8,128)} %bitcast.13), custom_call_target="tpu_custom_call" | custom-call | tf_op jit(solution)/shard_map/pallas_call | solution.py:293
  6.3 0.0 copy-start.4
  6.3 0.0 copy-start.5
  6.3 16.7 %all-to-all-start = ((f32[256,4,8,128]{3,2,1,0:T(8,128)}), f32[256,4,8,128]{3,2,1,0:T(8,128)}, u32[]{:S(2)}, u32[]{:S(2)}) async-start(f32[256,4,8,128]{3,2,1,0:T(8,128)} %bitcast.12), calls=%async_computation | async-start | bytes 8388608 | tf_op jit(solution)/shard_map/all_to_all | solution.py:306
  23.0 0.0 copy-done.4
  23.0 0.8 copy.8
  23.8 0.0 copy-done.5
  23.8 0.8 copy.9
  24.7 9.2 %shard_map.59 = (f32[128,512]{1,0:T(8,128)}, f32[128,512]{1,0:T(8,128)}) custom-call(s32[1]{0:T(128)} %bitcast.core_ref, s32[128,512]{1,0:T(8,128)} %bitcast.20, s32[128,512]{1,0:T(8,128)} %bitcast.21), custom_call_target="tpu_custom_call" | custom-call | tf_op jit(solution)/shard_map/pallas_call | solution.py:307
  33.9 85.6 %all-to-all-done = f32[256,4,8,128]{3,2,1,0:T(8,128)} async-done(((f32[256,4,8,128]{3,2,1,0:T(8,128)}), f32[256,4,8,128]{3,2,1,0:T(8,128)}, u32[]{:S(2)}, u32[]{:S(2)}) %all-to-all-start) | async-done | bytes 4194336 | tf_op jit(solution)/shard_map/all_to_all | solution.py:306
  119.5 6.3 %shard_map.60 = (f32[80,8,128]{2,1,0:T(8,128)}, f32[80,8,128]{2,1,0:T(8,128)}, bf16[512,2048]{1,0:T(8,128)(2,1)}, bf16[512,2048]{1,0:T(8,128)(2,1)}) custom-call(s32[1]{0:T(128)} %bitcast.core_ref, f32[32,8,4,8,128]{4,3,2,1,0:T(8,128)} %bitcast.5.fibers_hbm), custom_call_target="tpu_custom_call" | custom-call | tf_op jit(solution)/shard_map/pallas_call | solution.py:316
  125.8 1.5 collective-permute-start
  127.4 1.5 collective-permute-done
  128.8 1.0 add.6
  129.9 11.9 %all_to_all.40 = f32[16,5,8,128]{3,2,1,0:T(8,128)S(1)} all-to-all(f32[16,5,8,128]{3,2,1,0:T(8,128)S(1)} %bitcast.16), channel_id=1, replica_groups=mesh['z'=8,'x'=4,'y'=4,'c'=2] {'x','y'}, dimensions={0} | all-to-all | bytes 655360 | tf_op jit(solution)/shard_map/all_to_all | solution.py:284
  141.8 10.8 %all_to_all.41 = f32[8,5,8,128]{3,2,1,0:T(8,128)S(1)} all-to-all(f32[8,5,8,128]{3,2,1,0:T(8,128)S(1)} %broadcast_in_dim.12), channel_id=1, replica_groups=mesh['z'=8,'x'=4,'y'=4,'c'=2] {'z'}, dimensions={0} | all-to-all | bytes 327680 | tf_op jit(solution)/shard_map/all_to_all | solution.py:285
  152.6 11.6 %all_to_all.42 = f32[16,5,8,128]{3,2,1,0:T(8,128)S(1)} all-to-all(f32[16,5,8,128]{3,2,1,0:T(8,128)S(1)} %broadcast_in_dim.13), channel_id=1, replica_groups=mesh['z'=8,'x'=4,'y'=4,'c'=2] {'x','y'}, dimensions={0} | all-to-all | bytes 655360 | tf_op jit(solution)/shard_map/all_to_all | solution.py:286
  164.2 0.0 copy-start.1
  164.2 4.0 %collective-permute-start.1 = (f32[80,8,128]{2,1,0:T(8,128)S(1)}, f32[80,8,128]{2,1,0:T(8,128)S(1)}, u32[]{:S(2)}, u32[]{:S(2)}) collective-permute-start(f32[80,8,128]{2,1,0:T(8,128)S(1)} %bitcast.18), channel_id=1, source_target_pairs={{0,1},{1,0},{2,3},{3,2},{4,5},{5,4},{6,7},{7,6},{8,9},{9,8},{10,11... | collective-permute-start | bytes 983048 | tf_op jit(solution)/shard_map/ppermute | solution.py:278
  168.2 1.3 collective-permute-done.1.other_ref
  169.5 0.0 copy-start.3
  169.5 0.0 copy-done.1
  169.5 0.7 copy-done.3
  170.2 23.4 %shard_map.61 = (f32[512,128]{1,0:T(8,128)}, f32[128,2048]{1,0:T(8,128)}, f32[80,8,128]{2,1,0:T(8,128)}, f32[80,8,128]{2,1,0:T(8,128)}) custom-call(s32[1]{0:T(128)} %bitcast.core_ref, f32[80,8,128]{2,1,0:T(8,128)} %bitcast.19, f32[80,8,128]{2,1,0:T(8,128)} %copy-done.3, f32[128,512]{1,0:T(8,128)} %get-tuple-element.23.start_ref, ...), custom_call_target="tpu_custom_call" | custom-call | tf_op jit(solution)/shard_map/pallas_call | solution.py:332
  193.6 0.5 collective-permute-start.2
  194.0 1.5 collective-permute-done.2
  195.5 1.0 add.7
  196.5 11.1 %all_to_all.43 = f32[16,5,8,128]{3,2,1,0:T(8,128)S(1)} all-to-all(f32[16,5,8,128]{3,2,1,0:T(8,128)S(1)} %bitcast.17), channel_id=1, replica_groups=mesh['z'=8,'x'=4,'y'=4,'c'=2] {'x','y'}, dimensions={0} | all-to-all | bytes 655360 | tf_op jit(solution)/shard_map/all_to_all | solution.py:284
  207.7 10.8 %all_to_all.44 = f32[8,5,8,128]{3,2,1,0:T(8,128)S(1)} all-to-all(f32[8,5,8,128]{3,2,1,0:T(8,128)S(1)} %broadcast_in_dim.14), channel_id=1, replica_groups=mesh['z'=8,'x'=4,'y'=4,'c'=2] {'z'}, dimensions={0} | all-to-all | bytes 327680 | tf_op jit(solution)/shard_map/all_to_all | solution.py:285
  218.5 11.5 %all_to_all.45 = f32[16,5,8,128]{3,2,1,0:T(8,128)S(1)} all-to-all(f32[16,5,8,128]{3,2,1,0:T(8,128)S(1)} %broadcast_in_dim.15), channel_id=1, replica_groups=mesh['z'=8,'x'=4,'y'=4,'c'=2] {'x','y'}, dimensions={0} | all-to-all | bytes 655360 | tf_op jit(solution)/shard_map/all_to_all | solution.py:286
  230.1 0.0 copy-start
  230.1 4.0 %collective-permute-start.3 = (f32[80,8,128]{2,1,0:T(8,128)S(1)}, f32[80,8,128]{2,1,0:T(8,128)S(1)}, u32[]{:S(2)}, u32[]{:S(2)}) collective-permute-start(f32[80,8,128]{2,1,0:T(8,128)S(1)} %bitcast.14), channel_id=1, source_target_pairs={{0,1},{1,0},{2,3},{3,2},{4,5},{5,4},{6,7},{7,6},{8,9},{9,8},{10,11... | collective-permute-start | bytes 983048 | tf_op jit(solution)/shard_map/ppermute | solution.py:278
  234.0 1.3 collective-permute-done.3.other_ref
  235.3 0.0 copy-start.2
  235.3 0.0 copy-done
  235.3 0.7 copy-done.2
  236.0 21.1 %shard_map.62 = (f32[512,128]{1,0:T(8,128)}, f32[512,128]{1,0:T(8,128)}) custom-call(s32[1]{0:T(128)} %bitcast.core_ref, f32[80,8,128]{2,1,0:T(8,128)} %bitcast.15, f32[80,8,128]{2,1,0:T(8,128)} %copy-done.2, f32[128,512]{1,0:T(8,128)} %get-tuple-element.29.start_ref, f32[128,2048]{1,0:T(8,128)} %get-tuple-element.30.reduced_hbm), custom_call_target="tpu_custom_call" | custom-call | tf_op jit(solution)/shard_map/pallas_call | solution.py:349
  257.1 21.9 %all_to_all.46 = f32[256,2,128]{2,1,0:T(2,128)} all-to-all(f32[256,2,128]{2,1,0:T(2,128)} %bitcast.23), channel_id=1, replica_groups=mesh['z'=8,'x'=4,'y'=4,'c'=2] {'z','x','y','c'}, dimensions={0} | all-to-all | bytes 524288 | tf_op jit(solution)/shard_map/all_to_all | solution.py:358
  279.0 1.8 shard_map.63
  (8 shorter events, 0.2 us)
Async XLA Ops:
  6.3 16.7 %copy-start.4 = (s32[512,128]{1,0:T(8,128)S(1)}, s32[512,128]{1,0:T(8,128)}, u32[]{:S(2)}) copy-start(s32[512,128]{1,0:T(8,128)} %param.4) | copy-start | bytes 786436
  6.3 17.5 %copy-start.5 = (s32[512,128]{1,0:T(8,128)S(1)}, s32[512,128]{1,0:T(8,128)}, u32[]{:S(2)}) copy-start(s32[512,128]{1,0:T(8,128)} %param.5) | copy-start | bytes 786436
  6.3 113.2 %all-to-all-start = ((f32[256,4,8,128]{3,2,1,0:T(8,128)}), f32[256,4,8,128]{3,2,1,0:T(8,128)}, u32[]{:S(2)}, u32[]{:S(2)}) async-start(f32[256,4,8,128]{3,2,1,0:T(8,128)} %bitcast.12), calls=%async_computation | async-start | bytes 8388608 | tf_op jit(solution)/shard_map/all_to_all | solution.py:306
  125.8 3.0 %collective-permute-start = (f32[80,8,128]{2,1,0:T(8,128)}, f32[80,8,128]{2,1,0:T(8,128)S(1)}, u32[]{:S(2)}, u32[]{:S(2)}) collective-permute-start(f32[80,8,128]{2,1,0:T(8,128)} %get-tuple-element.22), channel_id=1, source_target_pairs={{0,1},{1,0},{2,3},{3,2},{4,5},{5,4},{6,7},{7,6},{8,9},{9,8},{10,11... | collective-permute-start | bytes 983048 | tf_op jit(solution)/shard_map/ppermute | solution.py:278
  164.2 5.3 %copy-start.1 = (f32[16,5,8,128]{3,2,1,0:T(8,128)}, f32[16,5,8,128]{3,2,1,0:T(8,128)S(1)}, u32[]{:S(2)}) copy-start(f32[16,5,8,128]{3,2,1,0:T(8,128)S(1)} %all_to_all.42) | copy-start | bytes 983044
  164.2 5.2 %collective-permute-start.1 = (f32[80,8,128]{2,1,0:T(8,128)S(1)}, f32[80,8,128]{2,1,0:T(8,128)S(1)}, u32[]{:S(2)}, u32[]{:S(2)}) collective-permute-start(f32[80,8,128]{2,1,0:T(8,128)S(1)} %bitcast.18), channel_id=1, source_target_pairs={{0,1},{1,0},{2,3},{3,2},{4,5},{5,4},{6,7},{7,6},{8,9},{9,8},{10,11... | collective-permute-start | bytes 983048 | tf_op jit(solution)/shard_map/ppermute | solution.py:278
  169.5 0.7 copy-start.3
  193.6 1.9 collective-permute-start.2
  230.1 5.3 %copy-start = (f32[16,5,8,128]{3,2,1,0:T(8,128)}, f32[16,5,8,128]{3,2,1,0:T(8,128)S(1)}, u32[]{:S(2)}) copy-start(f32[16,5,8,128]{3,2,1,0:T(8,128)S(1)} %all_to_all.45) | copy-start | bytes 983044
  230.1 5.2 %collective-permute-start.3 = (f32[80,8,128]{2,1,0:T(8,128)S(1)}, f32[80,8,128]{2,1,0:T(8,128)S(1)}, u32[]{:S(2)}, u32[]{:S(2)}) collective-permute-start(f32[80,8,128]{2,1,0:T(8,128)S(1)} %bitcast.14), channel_id=1, source_target_pairs={{0,1},{1,0},{2,3},{3,2},{4,5},{5,4},{6,7},{7,6},{8,9},{9,8},{10,11... | collective-permute-start | bytes 983048 | tf_op jit(solution)/shard_map/ppermute | solution.py:278
  235.3 0.7 copy-start.2

commit v5 on v4

--- a/solution.py
+++ b/solution.py
@@ -168,17 +168,11 @@
         save.wait()
 
 
-def leading(core_ref, mine_hbm, other_hbm, start_ref, whole, gram, parts, tile_sems):
+def leading(core_ref, mine_ref, other_ref, start_ref, whole, gram, parts):
     core = core_ref[0]
     one = ones(core_ref)
-    copies = [
-        pltpu.make_async_copy(mine_hbm, whole.at[core], tile_sems.at[0]),
-        pltpu.make_async_copy(other_hbm, whole.at[1 - core], tile_sems.at[1]),
-    ]
-    for copy in copies:
-        copy.start()
-    for copy in copies:
-        copy.wait()
+    whole[core] = mine_ref[...]
+    whole[1 - core] = other_ref[...]
     for at, (row, col) in enumerate(TILES):
         gram[8 * row : 8 * row + 8, 128 * col : 128 * col + 128] = whole[at // HALF, at % HALF]
     for row in range(1, 4):
@@ -197,12 +191,12 @@
 def first_basis_kernel(
     core_ref, mine_ref, other_ref, start_ref, high_hbm, low_hbm,
     basis_ref, reduced_ref, mine_out, other_out,
-    whole, gram, parts, tile_sems, held, high, low, turned_high, turned_low, sems,
+    whole, gram, parts, held, high, low, turned_high, turned_low, sems,
 ):
     copies = [pltpu.make_async_copy(high_hbm, high, sems.at[0]), pltpu.make_async_copy(low_hbm, low, sems.at[1])]
     for copy in copies:
         copy.start()
-    basis = leading(core_ref, mine_ref, other_ref, start_ref, whole, gram, parts, tile_sems)
+    basis = leading(core_ref, mine_ref, other_ref, start_ref, whole, gram, parts)
     basis_ref[...] = basis.T
     columns = []
     for k in range(4):
@@ -224,16 +218,10 @@
     upper_gram(turned_high, turned_low, mine_out, other_out, whole, core_ref[0])
 
 
-def second_basis_kernel(
-    core_ref, mine_ref, other_ref, start_ref, reduced_hbm, basis_ref, core_out,
-    whole, gram, parts, tile_sems, reduced, product, sem
-):
-    copy = pltpu.make_async_copy(reduced_hbm, reduced, sem)
-    copy.start()
-    basis = leading(core_ref, mine_ref, other_ref, start_ref, whole, gram, parts, tile_sems)
+def second_basis_kernel(core_ref, mine_ref, other_ref, start_ref, reduced, basis_ref, core_out, whole, gram, parts, product):
+    basis = leading(core_ref, mine_ref, other_ref, start_ref, whole, gram, parts)
     basis_ref[...] = basis.T
     basis = as_right_cols(basis)
-    copy.wait()
     for p in range(4):
         product[128 * p : 128 * p + 128, :] = dot(as_left(reduced[:, 512 * p : 512 * p + 512]), basis, NT)
     row = lax.broadcasted_iota(jnp.int32, (8, 128), 0)
@@ -270,8 +258,11 @@
     pltpu.VMEM((2, HALF, 8, 128), F32),
     pltpu.VMEM((N, N), F32),
     pltpu.VMEM((3 * N, N), BF16),
-    pltpu.SemaphoreType.DMA((2,)),
 ]
+
+
+def in_vmem(x):
+    return pltpu.with_memory_space_constraint(x, pltpu.VMEM)
 
 
 def across_cores(x):
@@ -285,7 +276,7 @@
     got = jnp.sum(lax.all_to_all(jnp.broadcast_to(got, (8, share, 8, 128)), "z", 0, 0, tiled=True), axis=0)
     got = lax.all_to_all(jnp.broadcast_to(got, (16, share, 8, 128)), ("x", "y"), 0, 0, tiled=True)
     got = got.reshape(HALF, 8, 128)
-    return got, across_cores(got)
+    return in_vmem(got), in_vmem(across_cores(got))
 
 
 def local(field, seeds_first, seeds_second):
@@ -306,13 +297,13 @@
     fibers = lax.all_to_all(sent.reshape(256, 4, 8, 128), ("z", "x", "y", "c"), 0, 0, tiled=True)
     starts = pl.pallas_call(
         seeds_kernel,
-        out_shape=(shaped(RANK, N), shaped(RANK, N)),
+        out_shape=(pltpu.VMEM((RANK, N), F32), pltpu.VMEM((RANK, N), F32)),
         in_specs=[SMEM, VMEM, VMEM],
         compiler_params=PARAMS,
     )(core, seeds_first.T, seeds_second.T)
     fibers, starts = lax.optimization_barrier((fibers, starts))
 
-    halves = (shaped(HALF, 8, 128), shaped(HALF, 8, 128))
+    halves = (pltpu.VMEM((HALF, 8, 128), F32), pltpu.VMEM((HALF, 8, 128), F32))
     mine, other, high, low = pl.pallas_call(
         first_gram_kernel,
         out_shape=halves + (shaped_half(N, 2048), shaped_half(N, 2048)),
@@ -331,8 +322,8 @@
     mine, other = total(mine, other)
     basis_first, reduced, mine, other = pl.pallas_call(
         first_basis_kernel,
-        out_shape=(shaped(N, RANK), shaped(RANK, 2048)) + halves,
-        in_specs=[SMEM, ANY, ANY, VMEM, ANY, ANY],
+        out_shape=(shaped(N, RANK), pltpu.VMEM((RANK, 2048), F32)) + halves,
+        in_specs=[SMEM, VMEM, VMEM, VMEM, ANY, ANY],
         out_specs=(VMEM, VMEM, VMEM, VMEM),
         scratch_shapes=LEADING_SCRATCH
         + [
@@ -344,20 +335,20 @@
             pltpu.SemaphoreType.DMA((2,)),
         ],
         compiler_params=PARAMS,
-    )(core, mine, other, starts[0], high, low)
+    )(core, mine, other, in_vmem(starts[0]), high, low)
     mine, other = total(mine, other)
     basis_second, ranks = pl.pallas_call(
         second_basis_kernel,
-        out_shape=(shaped(N, RANK), shaped(512, 128)),
-        in_specs=[SMEM, ANY, ANY, VMEM, ANY],
+        out_shape=(shaped(N, RANK), pltpu.VMEM((512, 128), F32)),
+        in_specs=[SMEM, VMEM, VMEM, VMEM, VMEM],
         out_specs=(VMEM, VMEM),
         scratch_shapes=LEADING_SCRATCH
-        + [pltpu.VMEM((RANK, 2048), F32), pltpu.VMEM((4 * RANK, RANK), F32), pltpu.SemaphoreType.DMA],
-        compiler_params=PARAMS,
-    )(core, mine, other, starts[1], reduced)
+        + [pltpu.VMEM((4 * RANK, RANK), F32)],
+        compiler_params=PARAMS,
+    )(core, mine, other, in_vmem(starts[1]), in_vmem(reduced))
     ranks = lax.all_to_all(ranks.reshape(256, 2, 128), ("z", "x", "y", "c"), 0, 0, tiled=True)
     core_tensor = pl.pallas_call(unpack_kernel, out_shape=shaped(4, 16, 1024), compiler_params=PARAMS)(
-        ranks.reshape(512, 128)
+        in_vmem(ranks.reshape(512, 128))
     )
     return (basis_first, basis_second, core_tensor)
 

time: 281 us -> 267 us (0.950)
  Pallas kernels: 67.4 us -> 58.2 us
    pallas_call x3, Pallas kernels: 53.7 us -> 46.3 us  [the longest x1 19.2 us: local(): pl.pallas_call(first_basis_kernel, out_shape=(shaped(N, RANK), pltpu.VMEM...]
where the time goes in v5:
time: 267 us
  waiting for transfers between devices  91.3 us (34%)
  blocking collectives  88.1 us (33%)
  Pallas kernels  58.2 us (22%)
  starting transfers between devices  26.6 us (10%)
    all_to_all x1, waiting for transfers between devices, local(): lax.all_to_all(sent.reshape(256, 4, 8, 128), ('z', 'x', 'y', 'c'), 0, 0,...  86.3 us
    all_to_all x2, blocking collectives, total(): lax.all_to_all(jnp.broadcast_to(got, (16, share, 8, 128)), ('x', 'y'), 0,...  23.2 us
    all_to_all x2, blocking collectives, total(): got = jnp.sum(lax.all_to_all(mine, ('x', 'y'), 0, 0, tiled=True), axis=0)  23 us
    all_to_all x2, blocking collectives, total(): lax.all_to_all(jnp.broadcast_to(got, (8, share, 8, 128)), 'z', 0, 0, tile...  21.5 us
    all_to_all x1, blocking collectives, local(): lax.all_to_all(ranks.reshape(256, 2, 128), ('z', 'x', 'y', 'c'), 0, 0, ti...  20.4 us
    pallas_call x1, Pallas kernels, local(): pl.pallas_call(first_basis_kernel, out_shape=(shaped(N, RANK), pltpu.VMEM...  19.2 us
    pallas_call x1, Pallas kernels, local(): pl.pallas_call(second_basis_kernel, out_shape=(shaped(N, RANK), pltpu.VME...  18.5 us
    all_to_all x1, starting transfers between devices, local(): lax.all_to_all(sent.reshape(256, 4, 8, 128), ('z', 'x', 'y', 'c'), 0, 0,...  16.7 us
  transfers between devices with their start and end apart: 5, of which 5 were waited for; matrix products, arithmetic and copies ran while one was open for 1% of the time, Pallas kernels for 3%

profile of v5, /device:TPU:1, one launch (start us, length us, event | category | flops | bytes accessed | tf_op | source)
XLA Modules:
  0.0 266.9 jit_solution(127029054235581977)
XLA Ops:
  0.6 5.7 %shard_map.58 = f32[2,128,4,8,128]{4,3,2,1,0:T(8,128)} custom-call(f32[2,8,64,1024]{3,2,1,0:T(8,128)} %bitcast.19), custom_call_target="tpu_custom_call" | custom-call | tf_op jit(solution)/shard_map/pallas_call | solution.py:284
  6.3 0.0 copy-start
  6.3 0.0 copy-start.1
  6.3 16.7 %all-to-all-start = ((f32[256,4,8,128]{3,2,1,0:T(8,128)}), f32[256,4,8,128]{3,2,1,0:T(8,128)}, u32[]{:S(2)}, u32[]{:S(2)}) async-start(f32[256,4,8,128]{3,2,1,0:T(8,128)} %bitcast.18), calls=%async_computation | async-start | bytes 8388608 | tf_op jit(solution)/shard_map/all_to_all | solution.py:297
  23.0 0.0 copy-done
  23.0 0.8 copy.8
  23.8 0.0 copy-done.1
  23.8 0.8 copy.9
  24.7 8.5 %shard_map.59 = (f32[128,512]{1,0:T(8,128)S(1)}, f32[128,512]{1,0:T(8,128)S(1)}) custom-call(s32[1]{0:T(128)} %bitcast.core_ref, s32[128,512]{1,0:T(8,128)} %bitcast.22, s32[128,512]{1,0:T(8,128)} %bitcast.23), custom_call_target="tpu_custom_call" | custom-call | tf_op jit(solution)/shard_map/pallas_call | solution.py:298
  33.2 86.3 %all-to-all-done = f32[256,4,8,128]{3,2,1,0:T(8,128)} async-done(((f32[256,4,8,128]{3,2,1,0:T(8,128)}), f32[256,4,8,128]{3,2,1,0:T(8,128)}, u32[]{:S(2)}, u32[]{:S(2)}) %all-to-all-start) | async-done | bytes 4194336 | tf_op jit(solution)/shard_map/all_to_all | solution.py:297
  119.5 5.4 %shard_map.60 = (f32[80,8,128]{2,1,0:T(8,128)S(1)}, f32[80,8,128]{2,1,0:T(8,128)S(1)}, bf16[512,2048]{1,0:T(8,128)(2,1)}, bf16[512,2048]{1,0:T(8,128)(2,1)}) custom-call(s32[1]{0:T(128)} %bitcast.core_ref, f32[32,8,4,8,128]{4,3,2,1,0:T(8,128)} %bitcast.5.fibers_hbm), custom_call_target="tpu_custom_call" | custom-call | tf_op jit(solution)/shard_map/pallas_call | solution.py:307
  125.0 1.5 collective-permute-start
  126.5 1.3 collective-permute-done
  127.8 11.9 %all_to_all.40 = f32[16,5,8,128]{3,2,1,0:T(8,128)S(1)} all-to-all(f32[16,5,8,128]{3,2,1,0:T(8,128)S(1)} %bitcast.20), channel_id=1, replica_groups=mesh['z'=8,'x'=4,'y'=4,'c'=2] {'x','y'}, dimensions={0} | all-to-all | bytes 655360 | tf_op jit(solution)/shard_map/all_to_all | solution.py:275
  139.7 10.8 %all_to_all.41 = f32[8,5,8,128]{3,2,1,0:T(8,128)S(1)} all-to-all(f32[8,5,8,128]{3,2,1,0:T(8,128)S(1)} %broadcast_in_dim.12), channel_id=1, replica_groups=mesh['z'=8,'x'=4,'y'=4,'c'=2] {'z'}, dimensions={0} | all-to-all | bytes 327680 | tf_op jit(solution)/shard_map/all_to_all | solution.py:276
  150.5 11.6 %all_to_all.42 = f32[16,5,8,128]{3,2,1,0:T(8,128)S(1)} all-to-all(f32[16,5,8,128]{3,2,1,0:T(8,128)S(1)} %broadcast_in_dim.13), channel_id=1, replica_groups=mesh['z'=8,'x'=4,'y'=4,'c'=2] {'x','y'}, dimensions={0} | all-to-all | bytes 655360 | tf_op jit(solution)/shard_map/all_to_all | solution.py:277
  162.1 4.0 %collective-permute-start.1 = (f32[80,8,128]{2,1,0:T(8,128)S(1)}, f32[80,8,128]{2,1,0:T(8,128)S(1)}, u32[]{:S(2)}, u32[]{:S(2)}) collective-permute-start(f32[80,8,128]{2,1,0:T(8,128)S(1)} %bitcast.14), channel_id=1, source_target_pairs={{0,1},{1,0},{2,3},{3,2},{4,5},{5,4},{6,7},{7,6},{8,9},{9,8},{10,11... | collective-permute-start | bytes 983048 | tf_op jit(solution)/shard_map/ppermute | solution.py:269
  166.1 1.3 collective-permute-done.1.other_ref
  167.4 19.2 %shard_map.61 = (f32[512,128]{1,0:T(8,128)}, f32[128,2048]{1,0:T(8,128)S(1)}, f32[80,8,128]{2,1,0:T(8,128)S(1)}, f32[80,8,128]{2,1,0:T(8,128)S(1)}) custom-call(s32[1]{0:T(128)} %bitcast.core_ref, f32[80,8,128]{2,1,0:T(8,128)S(1)} %bitcast.15, f32[80,8,128]{2,1,0:T(8,128)S(1)} %collective-permute-done.1.other_ref, ...), custom_call_target="tpu_custom_call" | custom-call | tf_op jit(solution)/shard_map/pallas_call | solution.py:323
  186.7 0.5 collective-permute-start.2
  187.1 1.3 collective-permute-done.2
  188.4 11.1 %all_to_all.43 = f32[16,5,8,128]{3,2,1,0:T(8,128)S(1)} all-to-all(f32[16,5,8,128]{3,2,1,0:T(8,128)S(1)} %bitcast.21), channel_id=1, replica_groups=mesh['z'=8,'x'=4,'y'=4,'c'=2] {'x','y'}, dimensions={0} | all-to-all | bytes 655360 | tf_op jit(solution)/shard_map/all_to_all | solution.py:275
  199.6 10.8 %all_to_all.44 = f32[8,5,8,128]{3,2,1,0:T(8,128)S(1)} all-to-all(f32[8,5,8,128]{3,2,1,0:T(8,128)S(1)} %broadcast_in_dim.14), channel_id=1, replica_groups=mesh['z'=8,'x'=4,'y'=4,'c'=2] {'z'}, dimensions={0} | all-to-all | bytes 327680 | tf_op jit(solution)/shard_map/all_to_all | solution.py:276
  210.4 11.5 %all_to_all.45 = f32[16,5,8,128]{3,2,1,0:T(8,128)S(1)} all-to-all(f32[16,5,8,128]{3,2,1,0:T(8,128)S(1)} %broadcast_in_dim.15), channel_id=1, replica_groups=mesh['z'=8,'x'=4,'y'=4,'c'=2] {'x','y'}, dimensions={0} | all-to-all | bytes 655360 | tf_op jit(solution)/shard_map/all_to_all | solution.py:277
  221.9 4.0 %collective-permute-start.3 = (f32[80,8,128]{2,1,0:T(8,128)S(1)}, f32[80,8,128]{2,1,0:T(8,128)S(1)}, u32[]{:S(2)}, u32[]{:S(2)}) collective-permute-start(f32[80,8,128]{2,1,0:T(8,128)S(1)} %bitcast.12), channel_id=1, source_target_pairs={{0,1},{1,0},{2,3},{3,2},{4,5},{5,4},{6,7},{7,6},{8,9},{9,8},{10,11... | collective-permute-start | bytes 983048 | tf_op jit(solution)/shard_map/ppermute | solution.py:269
  225.9 1.3 collective-permute-done.3.other_ref
  227.2 18.5 %shard_map.62 = (f32[512,128]{1,0:T(8,128)}, f32[512,128]{1,0:T(8,128)S(1)}) custom-call(s32[1]{0:T(128)} %bitcast.core_ref, f32[80,8,128]{2,1,0:T(8,128)S(1)} %bitcast.13, f32[80,8,128]{2,1,0:T(8,128)S(1)} %collective-permute-done.3.other_ref, f32[128,512]{1,0:T(8,128)S(1)} %get-tuple-element.29.start_ref, f32[128,2048]{1,0:T(8,128)S(1)} %get-tuple-element.30.reduced), custom_call_target="tpu_custom_call" | custom-call | tf_op jit(solution)/shard_map/pallas_call | solution.py:340
  245.7 20.4 %all_to_all.46 = f32[256,2,128]{2,1,0:T(2,128)S(1)} all-to-all(f32[256,2,128]{2,1,0:T(2,128)S(1)} %bitcast.17), channel_id=1, replica_groups=mesh['z'=8,'x'=4,'y'=4,'c'=2] {'z','x','y','c'}, dimensions={0} | all-to-all | bytes 524288 | tf_op jit(solution)/shard_map/all_to_all | solution.py:349
  266.1 0.8 shard_map.63
  (10 shorter events, 0.2 us)
Async XLA Ops:
  6.3 16.7 %copy-start = (s32[512,128]{1,0:T(8,128)S(1)}, s32[512,128]{1,0:T(8,128)}, u32[]{:S(2)}) copy-start(s32[512,128]{1,0:T(8,128)} %param.4) | copy-start | bytes 786436
  6.3 17.5 %copy-start.1 = (s32[512,128]{1,0:T(8,128)S(1)}, s32[512,128]{1,0:T(8,128)}, u32[]{:S(2)}) copy-start(s32[512,128]{1,0:T(8,128)} %param.5) | copy-start | bytes 786436
  6.3 113.2 %all-to-all-start = ((f32[256,4,8,128]{3,2,1,0:T(8,128)}), f32[256,4,8,128]{3,2,1,0:T(8,128)}, u32[]{:S(2)}, u32[]{:S(2)}) async-start(f32[256,4,8,128]{3,2,1,0:T(8,128)} %bitcast.18), calls=%async_computation | async-start | bytes 8388608 | tf_op jit(solution)/shard_map/all_to_all | solution.py:297
  125.0 2.8 %collective-permute-start = (f32[80,8,128]{2,1,0:T(8,128)S(1)}, f32[80,8,128]{2,1,0:T(8,128)S(1)}, u32[]{:S(2)}, u32[]{:S(2)}) collective-permute-start(f32[80,8,128]{2,1,0:T(8,128)S(1)} %get-tuple-element.22), channel_id=1, source_target_pairs={{0,1},{1,0},{2,3},{3,2},{4,5},{5,4},{6,7},{7,6},{8,9},{9,8},{10,11... | collective-permute-start | bytes 983048 | tf_op jit(solution)/shard_map/ppermute | solution.py:269
  162.1 5.3 %collective-permute-start.1 = (f32[80,8,128]{2,1,0:T(8,128)S(1)}, f32[80,8,128]{2,1,0:T(8,128)S(1)}, u32[]{:S(2)}, u32[]{:S(2)}) collective-permute-start(f32[80,8,128]{2,1,0:T(8,128)S(1)} %bitcast.14), channel_id=1, source_target_pairs={{0,1},{1,0},{2,3},{3,2},{4,5},{5,4},{6,7},{7,6},{8,9},{9,8},{10,11... | collective-permute-start | bytes 983048 | tf_op jit(solution)/shard_map/ppermute | solution.py:269
  186.7 1.7 collective-permute-start.2
  221.9 5.2 %collective-permute-start.3 = (f32[80,8,128]{2,1,0:T(8,128)S(1)}, f32[80,8,128]{2,1,0:T(8,128)S(1)}, u32[]{:S(2)}, u32[]{:S(2)}) collective-permute-start(f32[80,8,128]{2,1,0:T(8,128)S(1)} %bitcast.12), channel_id=1, source_target_pairs={{0,1},{1,0},{2,3},{3,2},{4,5},{5,4},{6,7},{7,6},{8,9},{9,8},{10,11... | collective-permute-start | bytes 983048 | tf_op jit(solution)/shard_map/ppermute | solution.py:269

commit v6 on v5

--- a/solution.py
+++ b/solution.py
@@ -52,10 +52,15 @@
     out = []
     for last in (8, 16):
         factor = []
+        ready = None
         for p in range(last - 8, last):
             rows = range(p, last)
-            cols = {i: [spread(rest[i][:, 8 * p + t : 8 * p + t + 1]) for t in range(8)] for i in rows}
-            cols[p] = [col * one for col in cols[p]]
+            column = lambda i, at: [spread(rest[i][:, at + t : at + t + 1]) for t in range(8)]
+            cols = {i: column(i, 8 * p) for i in rows[1:]}
+            cols[p] = ready or [col * one for col in column(p, 8 * p)]
+            coming = {}
+            if p + 1 < last:
+                coming = {p: [col * one for col in column(p, 8 * p + 8)], p + 1: column(p + 1, 8 * p + 8)}
             panel = (lane >= 8 * p) & (lane < 8 * p + 8)
             for i in rows:
                 unit = jnp.where(lane == sub + 8 * p, 1.0, 0.0) if i == p else 0.0
@@ -69,12 +74,16 @@
                 pivots = jnp.where(sub == t, pivot, pivots)
                 inverse = 1.0 / pivot
                 ahead = [spread(cols[p][u][t : t + 1, :]) for u in range(t + 1, 8)]
+                further = [spread(col[t : t + 1, :]) for col in coming[p]] if coming else []
                 for i in rows:
                     scaled = cols[i][t] * inverse
                     for k, u in enumerate(range(t + 1, 8)):
                         cols[i][u] = cols[i][u] - scaled * ahead[k]
+                    if i in coming and (i > p or t < 7):
+                        coming[i] = [col - scaled * more for col, more in zip(coming[i], further)]
                     if i > p or t < 7:
                         rest[i] = rest[i] - scaled * row
+            ready = coming.get(p + 1)
             done = done * lax.rsqrt(pivots)
             out.append(jnp.where(lane < 8 * p + 8, done, 0.0))
             factor.append(jnp.where((lane < 8 * p + 8) | (lane >= 8 * last), done, 0.0))

time: 267 us -> 261 us (0.978)
  Pallas kernels: 58.2 us -> 50 us
    pallas_call x1, Pallas kernels: 18.5 us -> 15.2 us  [local(): pl.pallas_call(second_basis_kernel, out_shape=(shaped(N, RANK), pltpu.VME...]
    pallas_call x1, Pallas kernels: 19.2 us -> 16 us  [local(): pl.pallas_call(first_basis_kernel, out_shape=(shaped(N, RANK), pltpu.VMEM...]
where the time goes in v6:
time: 261 us; the launch traced here: 260 us
  waiting for transfers between devices  93 us (36%)
  blocking collectives  88.1 us (34%)
  Pallas kernels  50 us (19%)
  starting transfers between devices  26.5 us (10%)
    all_to_all x1, waiting for transfers between devices, local(): lax.all_to_all(sent.reshape(256, 4, 8, 128), ('z', 'x', 'y', 'c'), 0, 0,...  88 us
    all_to_all x2, blocking collectives, total(): lax.all_to_all(jnp.broadcast_to(got, (16, share, 8, 128)), ('x', 'y'), 0,...  23.2 us
    all_to_all x2, blocking collectives, total(): got = jnp.sum(lax.all_to_all(mine, ('x', 'y'), 0, 0, tiled=True), axis=0)  23 us
    all_to_all x2, blocking collectives, total(): lax.all_to_all(jnp.broadcast_to(got, (8, share, 8, 128)), 'z', 0, 0, tile...  21.5 us
    all_to_all x1, blocking collectives, local(): lax.all_to_all(ranks.reshape(256, 2, 128), ('z', 'x', 'y', 'c'), 0, 0, ti...  20.4 us
    all_to_all x1, starting transfers between devices, local(): lax.all_to_all(sent.reshape(256, 4, 8, 128), ('z', 'x', 'y', 'c'), 0, 0,...  16.7 us
    pallas_call x1, Pallas kernels, local(): pl.pallas_call(first_basis_kernel, out_shape=(shaped(N, RANK), pltpu.VMEM...  16 us
    pallas_call x1, Pallas kernels, local(): pl.pallas_call(second_basis_kernel, out_shape=(shaped(N, RANK), pltpu.VME...  15.2 us
  transfers between devices with their start and end apart: 5, of which 5 were waited for; matrix products, arithmetic and copies ran while one was open for 1% of the time, Pallas kernels for 3%

profile of v6, /device:TPU:1, one launch (start us, length us, event | category | flops | bytes accessed | tf_op | source)
XLA Modules:
  0.0 260.2 jit_solution(10106739954844853785)
XLA Ops:
  0.6 5.7 %shard_map.58 = f32[2,128,4,8,128]{4,3,2,1,0:T(8,128)} custom-call(f32[2,8,64,1024]{3,2,1,0:T(8,128)} %bitcast.19), custom_call_target="tpu_custom_call" | custom-call | tf_op jit(solution)/shard_map/pallas_call | solution.py:293
  6.3 0.0 copy-start
  6.3 0.0 copy-start.1
  6.3 16.7 %all-to-all-start = ((f32[256,4,8,128]{3,2,1,0:T(8,128)}), f32[256,4,8,128]{3,2,1,0:T(8,128)}, u32[]{:S(2)}, u32[]{:S(2)}) async-start(f32[256,4,8,128]{3,2,1,0:T(8,128)} %bitcast.18), calls=%async_computation | async-start | bytes 8388608 | tf_op jit(solution)/shard_map/all_to_all | solution.py:306
  23.0 0.0 copy-done
  23.0 0.8 copy.8
  23.9 0.0 copy-done.1
  23.9 0.8 copy.9
  24.7 6.9 %shard_map.59 = (f32[128,512]{1,0:T(8,128)S(1)}, f32[128,512]{1,0:T(8,128)S(1)}) custom-call(s32[1]{0:T(128)} %bitcast.core_ref, s32[128,512]{1,0:T(8,128)} %bitcast.22, s32[128,512]{1,0:T(8,128)} %bitcast.23), custom_call_target="tpu_custom_call" | custom-call | tf_op jit(solution)/shard_map/pallas_call | solution.py:307
  31.6 88.0 %all-to-all-done = f32[256,4,8,128]{3,2,1,0:T(8,128)} async-done(((f32[256,4,8,128]{3,2,1,0:T(8,128)}), f32[256,4,8,128]{3,2,1,0:T(8,128)}, u32[]{:S(2)}, u32[]{:S(2)}) %all-to-all-start) | async-done | bytes 4194336 | tf_op jit(solution)/shard_map/all_to_all | solution.py:306
  119.5 5.4 %shard_map.60 = (f32[80,8,128]{2,1,0:T(8,128)S(1)}, f32[80,8,128]{2,1,0:T(8,128)S(1)}, bf16[512,2048]{1,0:T(8,128)(2,1)}, bf16[512,2048]{1,0:T(8,128)(2,1)}) custom-call(s32[1]{0:T(128)} %bitcast.core_ref, f32[32,8,4,8,128]{4,3,2,1,0:T(8,128)} %bitcast.5.fibers_hbm), custom_call_target="tpu_custom_call" | custom-call | tf_op jit(solution)/shard_map/pallas_call | solution.py:316
  125.0 1.4 collective-permute-start
  126.3 1.3 collective-permute-done
  127.6 11.9 %all_to_all.40 = f32[16,5,8,128]{3,2,1,0:T(8,128)S(1)} all-to-all(f32[16,5,8,128]{3,2,1,0:T(8,128)S(1)} %bitcast.20), channel_id=1, replica_groups=mesh['z'=8,'x'=4,'y'=4,'c'=2] {'x','y'}, dimensions={0} | all-to-all | bytes 655360 | tf_op jit(solution)/shard_map/all_to_all | solution.py:284
  139.5 10.8 %all_to_all.41 = f32[8,5,8,128]{3,2,1,0:T(8,128)S(1)} all-to-all(f32[8,5,8,128]{3,2,1,0:T(8,128)S(1)} %broadcast_in_dim.12), channel_id=1, replica_groups=mesh['z'=8,'x'=4,'y'=4,'c'=2] {'z'}, dimensions={0} | all-to-all | bytes 327680 | tf_op jit(solution)/shard_map/all_to_all | solution.py:285
  150.3 11.6 %all_to_all.42 = f32[16,5,8,128]{3,2,1,0:T(8,128)S(1)} all-to-all(f32[16,5,8,128]{3,2,1,0:T(8,128)S(1)} %broadcast_in_dim.13), channel_id=1, replica_groups=mesh['z'=8,'x'=4,'y'=4,'c'=2] {'x','y'}, dimensions={0} | all-to-all | bytes 655360 | tf_op jit(solution)/shard_map/all_to_all | solution.py:286
  162.0 4.0 %collective-permute-start.1 = (f32[80,8,128]{2,1,0:T(8,128)S(1)}, f32[80,8,128]{2,1,0:T(8,128)S(1)}, u32[]{:S(2)}, u32[]{:S(2)}) collective-permute-start(f32[80,8,128]{2,1,0:T(8,128)S(1)} %bitcast.14), channel_id=1, source_target_pairs={{0,1},{1,0},{2,3},{3,2},{4,5},{5,4},{6,7},{7,6},{8,9},{9,8},{10,11... | collective-permute-start | bytes 983048 | tf_op jit(solution)/shard_map/ppermute | solution.py:278
  166.0 1.3 collective-permute-done.1.other_ref
  167.2 16.0 %shard_map.61 = (f32[512,128]{1,0:T(8,128)}, f32[128,2048]{1,0:T(8,128)S(1)}, f32[80,8,128]{2,1,0:T(8,128)S(1)}, f32[80,8,128]{2,1,0:T(8,128)S(1)}) custom-call(s32[1]{0:T(128)} %bitcast.core_ref, f32[80,8,128]{2,1,0:T(8,128)S(1)} %bitcast.15, f32[80,8,128]{2,1,0:T(8,128)S(1)} %collective-permute-done.1.other_ref, ...), custom_call_target="tpu_custom_call" | custom-call | tf_op jit(solution)/shard_map/pallas_call | solution.py:332
  183.2 0.5 collective-permute-start.2
  183.7 1.3 collective-permute-done.2
  185.0 11.1 %all_to_all.43 = f32[16,5,8,128]{3,2,1,0:T(8,128)S(1)} all-to-all(f32[16,5,8,128]{3,2,1,0:T(8,128)S(1)} %bitcast.21), channel_id=1, replica_groups=mesh['z'=8,'x'=4,'y'=4,'c'=2] {'x','y'}, dimensions={0} | all-to-all | bytes 655360 | tf_op jit(solution)/shard_map/all_to_all | solution.py:284
  196.2 10.8 %all_to_all.44 = f32[8,5,8,128]{3,2,1,0:T(8,128)S(1)} all-to-all(f32[8,5,8,128]{3,2,1,0:T(8,128)S(1)} %broadcast_in_dim.14), channel_id=1, replica_groups=mesh['z'=8,'x'=4,'y'=4,'c'=2] {'z'}, dimensions={0} | all-to-all | bytes 327680 | tf_op jit(solution)/shard_map/all_to_all | solution.py:285
  207.0 11.5 %all_to_all.45 = f32[16,5,8,128]{3,2,1,0:T(8,128)S(1)} all-to-all(f32[16,5,8,128]{3,2,1,0:T(8,128)S(1)} %broadcast_in_dim.15), channel_id=1, replica_groups=mesh['z'=8,'x'=4,'y'=4,'c'=2] {'x','y'}, dimensions={0} | all-to-all | bytes 655360 | tf_op jit(solution)/shard_map/all_to_all | solution.py:286
  218.5 4.0 %collective-permute-start.3 = (f32[80,8,128]{2,1,0:T(8,128)S(1)}, f32[80,8,128]{2,1,0:T(8,128)S(1)}, u32[]{:S(2)}, u32[]{:S(2)}) collective-permute-start(f32[80,8,128]{2,1,0:T(8,128)S(1)} %bitcast.12), channel_id=1, source_target_pairs={{0,1},{1,0},{2,3},{3,2},{4,5},{5,4},{6,7},{7,6},{8,9},{9,8},{10,11... | collective-permute-start | bytes 983048 | tf_op jit(solution)/shard_map/ppermute | solution.py:278
  222.5 1.3 collective-permute-done.3.other_ref
  223.8 15.2 %shard_map.62 = (f32[512,128]{1,0:T(8,128)}, f32[512,128]{1,0:T(8,128)S(1)}) custom-call(s32[1]{0:T(128)} %bitcast.core_ref, f32[80,8,128]{2,1,0:T(8,128)S(1)} %bitcast.13, f32[80,8,128]{2,1,0:T(8,128)S(1)} %collective-permute-done.3.other_ref, f32[128,512]{1,0:T(8,128)S(1)} %get-tuple-element.29.start_ref, f32[128,2048]{1,0:T(8,128)S(1)} %get-tuple-element.30.reduced), custom_call_target="tpu_custom_call" | custom-call | tf_op jit(solution)/shard_map/pallas_call | solution.py:349
  238.9 20.4 %all_to_all.46 = f32[256,2,128]{2,1,0:T(2,128)S(1)} all-to-all(f32[256,2,128]{2,1,0:T(2,128)S(1)} %bitcast.17), channel_id=1, replica_groups=mesh['z'=8,'x'=4,'y'=4,'c'=2] {'z','x','y','c'}, dimensions={0} | all-to-all | bytes 524288 | tf_op jit(solution)/shard_map/all_to_all | solution.py:358
  259.4 0.8 shard_map.63
  (10 shorter events, 0.2 us)
Async XLA Ops:
  6.3 16.7 %copy-start = (s32[512,128]{1,0:T(8,128)S(1)}, s32[512,128]{1,0:T(8,128)}, u32[]{:S(2)}) copy-start(s32[512,128]{1,0:T(8,128)} %param.4) | copy-start | bytes 786436
  6.3 17.5 %copy-start.1 = (s32[512,128]{1,0:T(8,128)S(1)}, s32[512,128]{1,0:T(8,128)}, u32[]{:S(2)}) copy-start(s32[512,128]{1,0:T(8,128)} %param.5) | copy-start | bytes 786436
  6.3 113.2 %all-to-all-start = ((f32[256,4,8,128]{3,2,1,0:T(8,128)}), f32[256,4,8,128]{3,2,1,0:T(8,128)}, u32[]{:S(2)}, u32[]{:S(2)}) async-start(f32[256,4,8,128]{3,2,1,0:T(8,128)} %bitcast.18), calls=%async_computation | async-start | bytes 8388608 | tf_op jit(solution)/shard_map/all_to_all | solution.py:306
  125.0 2.6 %collective-permute-start = (f32[80,8,128]{2,1,0:T(8,128)S(1)}, f32[80,8,128]{2,1,0:T(8,128)S(1)}, u32[]{:S(2)}, u32[]{:S(2)}) collective-permute-start(f32[80,8,128]{2,1,0:T(8,128)S(1)} %get-tuple-element.22), channel_id=1, source_target_pairs={{0,1},{1,0},{2,3},{3,2},{4,5},{5,4},{6,7},{7,6},{8,9},{9,8},{10,11... | collective-permute-start | bytes 983048 | tf_op jit(solution)/shard_map/ppermute | solution.py:278
  162.0 5.3 %collective-permute-start.1 = (f32[80,8,128]{2,1,0:T(8,128)S(1)}, f32[80,8,128]{2,1,0:T(8,128)S(1)}, u32[]{:S(2)}, u32[]{:S(2)}) collective-permute-start(f32[80,8,128]{2,1,0:T(8,128)S(1)} %bitcast.14), channel_id=1, source_target_pairs={{0,1},{1,0},{2,3},{3,2},{4,5},{5,4},{6,7},{7,6},{8,9},{9,8},{10,11... | collective-permute-start | bytes 983048 | tf_op jit(solution)/shard_map/ppermute | solution.py:278
  183.2 1.7 collective-permute-start.2
  218.5 5.2 %collective-permute-start.3 = (f32[80,8,128]{2,1,0:T(8,128)S(1)}, f32[80,8,128]{2,1,0:T(8,128)S(1)}, u32[]{:S(2)}, u32[]{:S(2)}) collective-permute-start(f32[80,8,128]{2,1,0:T(8,128)S(1)} %bitcast.12), channel_id=1, source_target_pairs={{0,1},{1,0},{2,3},{3,2},{4,5},{5,4},{6,7},{7,6},{8,9},{9,8},{10,11... | collective-permute-start | bytes 983048 | tf_op jit(solution)/shard_map/ppermute | solution.py:278

commit v7 on v6

--- a/solution.py
+++ b/solution.py
@@ -89,12 +89,11 @@
             factor.append(jnp.where((lane < 8 * p + 8) | (lane >= 8 * last), done, 0.0))
         if last < 16:
             factor = jnp.concatenate(factor, axis=0)
-            change = lax.dot_general(
-                factor[:, 8 * last :],
-                factor,
+            high, low = split(factor)
+            change = dot(
+                jnp.concatenate([high, low, high], axis=0)[:, 8 * last :],
+                jnp.concatenate([high, high, low], axis=0),
                 (((0,), (0,)), ((), ())),
-                precision=lax.Precision.HIGHEST,
-                preferred_element_type=F32,
             )
             for k, i in enumerate(range(last, 16)):
                 rest[i] = jnp.where(lane < 8 * last, 0.0, rest[i]) - change[8 * k : 8 * k + 8]

time: 261 us -> 260 us (level)
  no operation moved by 1% of the time
where the time goes in v7:
time: 260 us
  waiting for transfers between devices  93.2 us (36%)
  blocking collectives  88.1 us (34%)
  Pallas kernels  49.1 us (19%)
  starting transfers between devices  26.5 us (10%)
    all_to_all x1, waiting for transfers between devices, local(): lax.all_to_all(sent.reshape(256, 4, 8, 128), ('z', 'x', 'y', 'c'), 0, 0,...  88.1 us
    all_to_all x2, blocking collectives, total(): lax.all_to_all(jnp.broadcast_to(got, (16, share, 8, 128)), ('x', 'y'), 0,...  23.2 us
    all_to_all x2, blocking collectives, total(): got = jnp.sum(lax.all_to_all(mine, ('x', 'y'), 0, 0, tiled=True), axis=0)  23 us
    all_to_all x2, blocking collectives, total(): lax.all_to_all(jnp.broadcast_to(got, (8, share, 8, 128)), 'z', 0, 0, tile...  21.5 us
    all_to_all x1, blocking collectives, local(): lax.all_to_all(ranks.reshape(256, 2, 128), ('z', 'x', 'y', 'c'), 0, 0, ti...  20.4 us
    all_to_all x1, starting transfers between devices, local(): lax.all_to_all(sent.reshape(256, 4, 8, 128), ('z', 'x', 'y', 'c'), 0, 0,...  16.7 us
    pallas_call x1, Pallas kernels, local(): pl.pallas_call(first_basis_kernel, out_shape=(shaped(N, RANK), pltpu.VMEM...  15.6 us
    pallas_call x1, Pallas kernels, local(): pl.pallas_call(second_basis_kernel, out_shape=(shaped(N, RANK), pltpu.VME...  14.9 us
  transfers between devices with their start and end apart: 5, of which 5 were waited for; matrix products, arithmetic and copies ran while one was open for 1% of the time, Pallas kernels for 3%

profile of v7, /device:TPU:1, one launch (start us, length us, event | category | flops | bytes accessed | tf_op | source)
XLA Modules:
  0.0 259.5 jit_solution(5529979220782661869)
XLA Ops:
  0.6 5.7 %shard_map.58 = f32[2,128,4,8,128]{4,3,2,1,0:T(8,128)} custom-call(f32[2,8,64,1024]{3,2,1,0:T(8,128)} %bitcast.19), custom_call_target="tpu_custom_call" | custom-call | tf_op jit(solution)/shard_map/pallas_call | solution.py:292
  6.3 0.0 copy-start
  6.3 0.0 copy-start.1
  6.3 16.7 %all-to-all-start = ((f32[256,4,8,128]{3,2,1,0:T(8,128)}), f32[256,4,8,128]{3,2,1,0:T(8,128)}, u32[]{:S(2)}, u32[]{:S(2)}) async-start(f32[256,4,8,128]{3,2,1,0:T(8,128)} %bitcast.18), calls=%async_computation | async-start | bytes 8388608 | tf_op jit(solution)/shard_map/all_to_all | solution.py:305
  23.0 0.0 copy-done
  23.0 0.8 copy.8
  23.9 0.0 copy-done.1
  23.9 0.8 copy.9
  24.7 6.7 %shard_map.59 = (f32[128,512]{1,0:T(8,128)S(1)}, f32[128,512]{1,0:T(8,128)S(1)}) custom-call(s32[1]{0:T(128)} %bitcast.core_ref, s32[128,512]{1,0:T(8,128)} %bitcast.22, s32[128,512]{1,0:T(8,128)} %bitcast.23), custom_call_target="tpu_custom_call" | custom-call | tf_op jit(solution)/shard_map/pallas_call | solution.py:306
  31.4 88.1 %all-to-all-done = f32[256,4,8,128]{3,2,1,0:T(8,128)} async-done(((f32[256,4,8,128]{3,2,1,0:T(8,128)}), f32[256,4,8,128]{3,2,1,0:T(8,128)}, u32[]{:S(2)}, u32[]{:S(2)}) %all-to-all-start) | async-done | bytes 4194336 | tf_op jit(solution)/shard_map/all_to_all | solution.py:305
  119.5 5.4 %shard_map.60 = (f32[80,8,128]{2,1,0:T(8,128)S(1)}, f32[80,8,128]{2,1,0:T(8,128)S(1)}, bf16[512,2048]{1,0:T(8,128)(2,1)}, bf16[512,2048]{1,0:T(8,128)(2,1)}) custom-call(s32[1]{0:T(128)} %bitcast.core_ref, f32[32,8,4,8,128]{4,3,2,1,0:T(8,128)} %bitcast.5.fibers_hbm), custom_call_target="tpu_custom_call" | custom-call | tf_op jit(solution)/shard_map/pallas_call | solution.py:315
  125.0 1.4 collective-permute-start
  126.3 1.3 collective-permute-done
  127.6 11.9 %all_to_all.40 = f32[16,5,8,128]{3,2,1,0:T(8,128)S(1)} all-to-all(f32[16,5,8,128]{3,2,1,0:T(8,128)S(1)} %bitcast.20), channel_id=1, replica_groups=mesh['z'=8,'x'=4,'y'=4,'c'=2] {'x','y'}, dimensions={0} | all-to-all | bytes 655360 | tf_op jit(solution)/shard_map/all_to_all | solution.py:283
  139.5 10.8 %all_to_all.41 = f32[8,5,8,128]{3,2,1,0:T(8,128)S(1)} all-to-all(f32[8,5,8,128]{3,2,1,0:T(8,128)S(1)} %broadcast_in_dim.12), channel_id=1, replica_groups=mesh['z'=8,'x'=4,'y'=4,'c'=2] {'z'}, dimensions={0} | all-to-all | bytes 327680 | tf_op jit(solution)/shard_map/all_to_all | solution.py:284
  150.3 11.6 %all_to_all.42 = f32[16,5,8,128]{3,2,1,0:T(8,128)S(1)} all-to-all(f32[16,5,8,128]{3,2,1,0:T(8,128)S(1)} %broadcast_in_dim.13), channel_id=1, replica_groups=mesh['z'=8,'x'=4,'y'=4,'c'=2] {'x','y'}, dimensions={0} | all-to-all | bytes 655360 | tf_op jit(solution)/shard_map/all_to_all | solution.py:285
  162.0 4.0 %collective-permute-start.1 = (f32[80,8,128]{2,1,0:T(8,128)S(1)}, f32[80,8,128]{2,1,0:T(8,128)S(1)}, u32[]{:S(2)}, u32[]{:S(2)}) collective-permute-start(f32[80,8,128]{2,1,0:T(8,128)S(1)} %bitcast.14), channel_id=1, source_target_pairs={{0,1},{1,0},{2,3},{3,2},{4,5},{5,4},{6,7},{7,6},{8,9},{9,8},{10,11... | collective-permute-start | bytes 983048 | tf_op jit(solution)/shard_map/ppermute | solution.py:277
  166.0 1.3 collective-permute-done.1.other_ref
  167.2 15.6 %shard_map.61 = (f32[512,128]{1,0:T(8,128)}, f32[128,2048]{1,0:T(8,128)S(1)}, f32[80,8,128]{2,1,0:T(8,128)S(1)}, f32[80,8,128]{2,1,0:T(8,128)S(1)}) custom-call(s32[1]{0:T(128)} %bitcast.core_ref, f32[80,8,128]{2,1,0:T(8,128)S(1)} %bitcast.15, f32[80,8,128]{2,1,0:T(8,128)S(1)} %collective-permute-done.1.other_ref, ...), custom_call_target="tpu_custom_call" | custom-call | tf_op jit(solution)/shard_map/pallas_call | solution.py:331
  182.9 0.5 collective-permute-start.2
  183.3 1.3 collective-permute-done.2
  184.6 11.1 %all_to_all.43 = f32[16,5,8,128]{3,2,1,0:T(8,128)S(1)} all-to-all(f32[16,5,8,128]{3,2,1,0:T(8,128)S(1)} %bitcast.21), channel_id=1, replica_groups=mesh['z'=8,'x'=4,'y'=4,'c'=2] {'x','y'}, dimensions={0} | all-to-all | bytes 655360 | tf_op jit(solution)/shard_map/all_to_all | solution.py:283
  195.8 10.8 %all_to_all.44 = f32[8,5,8,128]{3,2,1,0:T(8,128)S(1)} all-to-all(f32[8,5,8,128]{3,2,1,0:T(8,128)S(1)} %broadcast_in_dim.14), channel_id=1, replica_groups=mesh['z'=8,'x'=4,'y'=4,'c'=2] {'z'}, dimensions={0} | all-to-all | bytes 327680 | tf_op jit(solution)/shard_map/all_to_all | solution.py:284
  206.6 11.5 %all_to_all.45 = f32[16,5,8,128]{3,2,1,0:T(8,128)S(1)} all-to-all(f32[16,5,8,128]{3,2,1,0:T(8,128)S(1)} %broadcast_in_dim.15), channel_id=1, replica_groups=mesh['z'=8,'x'=4,'y'=4,'c'=2] {'x','y'}, dimensions={0} | all-to-all | bytes 655360 | tf_op jit(solution)/shard_map/all_to_all | solution.py:285
  218.2 4.0 %collective-permute-start.3 = (f32[80,8,128]{2,1,0:T(8,128)S(1)}, f32[80,8,128]{2,1,0:T(8,128)S(1)}, u32[]{:S(2)}, u32[]{:S(2)}) collective-permute-start(f32[80,8,128]{2,1,0:T(8,128)S(1)} %bitcast.12), channel_id=1, source_target_pairs={{0,1},{1,0},{2,3},{3,2},{4,5},{5,4},{6,7},{7,6},{8,9},{9,8},{10,11... | collective-permute-start | bytes 983048 | tf_op jit(solution)/shard_map/ppermute | solution.py:277
  222.1 1.3 collective-permute-done.3.other_ref
  223.4 14.9 %shard_map.62 = (f32[512,128]{1,0:T(8,128)}, f32[512,128]{1,0:T(8,128)S(1)}) custom-call(s32[1]{0:T(128)} %bitcast.core_ref, f32[80,8,128]{2,1,0:T(8,128)S(1)} %bitcast.13, f32[80,8,128]{2,1,0:T(8,128)S(1)} %collective-permute-done.3.other_ref, f32[128,512]{1,0:T(8,128)S(1)} %get-tuple-element.29.start_ref, f32[128,2048]{1,0:T(8,128)S(1)} %get-tuple-element.30.reduced), custom_call_target="tpu_custom_call" | custom-call | tf_op jit(solution)/shard_map/pallas_call | solution.py:348
  238.3 20.4 %all_to_all.46 = f32[256,2,128]{2,1,0:T(2,128)S(1)} all-to-all(f32[256,2,128]{2,1,0:T(2,128)S(1)} %bitcast.17), channel_id=1, replica_groups=mesh['z'=8,'x'=4,'y'=4,'c'=2] {'z','x','y','c'}, dimensions={0} | all-to-all | bytes 524288 | tf_op jit(solution)/shard_map/all_to_all | solution.py:357
  258.7 0.8 shard_map.63
  (10 shorter events, 0.2 us)
Async XLA Ops:
  6.3 16.7 %copy-start = (s32[512,128]{1,0:T(8,128)S(1)}, s32[512,128]{1,0:T(8,128)}, u32[]{:S(2)}) copy-start(s32[512,128]{1,0:T(8,128)} %param.4) | copy-start | bytes 786436
  6.3 17.5 %copy-start.1 = (s32[512,128]{1,0:T(8,128)S(1)}, s32[512,128]{1,0:T(8,128)}, u32[]{:S(2)}) copy-start(s32[512,128]{1,0:T(8,128)} %param.5) | copy-start | bytes 786436
  6.3 113.2 %all-to-all-start = ((f32[256,4,8,128]{3,2,1,0:T(8,128)}), f32[256,4,8,128]{3,2,1,0:T(8,128)}, u32[]{:S(2)}, u32[]{:S(2)}) async-start(f32[256,4,8,128]{3,2,1,0:T(8,128)} %bitcast.18), calls=%async_computation | async-start | bytes 8388608 | tf_op jit(solution)/shard_map/all_to_all | solution.py:305
  125.0 2.6 %collective-permute-start = (f32[80,8,128]{2,1,0:T(8,128)S(1)}, f32[80,8,128]{2,1,0:T(8,128)S(1)}, u32[]{:S(2)}, u32[]{:S(2)}) collective-permute-start(f32[80,8,128]{2,1,0:T(8,128)S(1)} %get-tuple-element.22), channel_id=1, source_target_pairs={{0,1},{1,0},{2,3},{3,2},{4,5},{5,4},{6,7},{7,6},{8,9},{9,8},{10,11... | collective-permute-start | bytes 983048 | tf_op jit(solution)/shard_map/ppermute | solution.py:277
  162.0 5.3 %collective-permute-start.1 = (f32[80,8,128]{2,1,0:T(8,128)S(1)}, f32[80,8,128]{2,1,0:T(8,128)S(1)}, u32[]{:S(2)}, u32[]{:S(2)}) collective-permute-start(f32[80,8,128]{2,1,0:T(8,128)S(1)} %bitcast.14), channel_id=1, source_target_pairs={{0,1},{1,0},{2,3},{3,2},{4,5},{5,4},{6,7},{7,6},{8,9},{9,8},{10,11... | collective-permute-start | bytes 983048 | tf_op jit(solution)/shard_map/ppermute | solution.py:277
  182.9 1.7 collective-permute-start.2
  218.2 5.2 %collective-permute-start.3 = (f32[80,8,128]{2,1,0:T(8,128)S(1)}, f32[80,8,128]{2,1,0:T(8,128)S(1)}, u32[]{:S(2)}, u32[]{:S(2)}) collective-permute-start(f32[80,8,128]{2,1,0:T(8,128)S(1)} %bitcast.12), channel_id=1, source_target_pairs={{0,1},{1,0},{2,3},{3,2},{4,5},{5,4},{6,7},{7,6},{8,9},{9,8},{10,11... | collective-permute-start | bytes 983048 | tf_op jit(solution)/shard_map/ppermute | solution.py:277
